TPU v7x, 768 devices: a whole 4x8x12 slice. The times are simulated.
768 devices in a mesh: space: 12 (over z), bal: 64 (over x, y, core).
Axes of the slice: x: 4, y: 8, z: 12, core: 2. Of those that a mesh axis runs over, the one named last changes fastest.
Arguments:
- panels: bfloat16 [12, 64, 1024, 1024], P('space', 'bal'), may hold values from -0.1875 to 0.1875
- enrich: int32 [12, 64], P('space', 'bal'), may hold values from 1 to 2
- compliance: float32 [12, 64, 1024], P('space', 'bal'), may hold values from 0.5 to 2
- loads: float32 [12, 64, 64, 1024], P('space', 'bal'), may hold values from -6 to 6
- face_maps: int32 [12, 64, 4, 256], P('space', 'bal'), may hold values from 0 to 255, each once within a row
- face_lengths: int32 [12, 64, 4], P('space', 'bal'), may hold values from 128 to 256, as said below
- contact: int32 [12, 64, 128], P('space', 'bal'), may hold values from 0 to 1023
Outputs:
- solution: float32 [12, 64, 64, 1024], P('space', 'bal')
- residual: float32 [12, 64, 64, 1024], P('space', 'bal')
- violation: float32 [64], replicated
Inputs may be any that keep to these rules, and one draw needn't show every extreme that they name: `face_maps`: each face's slot-to-row table is a permutation of its 256 rows. `face_lengths`: the two faces of one shared interface have the same length; some face has all 256 slots live.
All inputs are finite; a program needn't handle non-finite values.
Results may differ from a plain program's by a relative error of at most 0.0003.
Values sent between devices are 32-bit elements; how exact they have to be, the bound alone decides.
No kernel may reach another device: no remote copies, remote signals or barrier semaphores. Data moves between devices by JAX's collectives and lax.ppermute only.
A program may use at most 32 MiB of HBM per device.

v0:
```python
import math

import jax
import jax.numpy as jnp
from jax import lax
from jax.sharding import PartitionSpec as P

IFACE = 1024
ROWS = 1024
BLOCK_ROWS = 512
ITERS = 3


def padded(block, sides, width):
    for axis, dim in sides:
        count = lax.axis_size(axis)
        forward = [(i, i + 1) for i in range(count - 1)]
        backward = [(target, source) for source, target in forward]
        low = lax.ppermute(
            lax.slice_in_dim(block, block.shape[dim] - width, None, axis=dim), axis, forward
        )
        high = lax.ppermute(lax.slice_in_dim(block, 0, width, axis=dim), axis, backward)
        block = jnp.concatenate([low, block, high], axis=dim)
    return block


def chebyshev_constants():
    upper = 2.6 * (1.0 + math.sqrt(IFACE / ROWS)) ** 2 + 4.0
    lower = 0.5
    center = (upper + lower) / 2.0
    half_span = (upper - lower) / 2.0
    return (center, half_span, center / half_span)


def canon_order(field, position):
    picked = jnp.take(field, position, axis=1)
    return jnp.moveaxis(picked, 1, 0)


def local_order(summed, inverse):
    face_rows = jnp.take_along_axis(summed, inverse[:, None, :], axis=2)
    return jnp.moveaxis(face_rows, 0, 1).reshape(summed.shape[1], -1)


def assemble(field, position, inverse):
    canonical = canon_order(field, position)
    along_space = padded(canonical[0:2], (("space", 0),), 1)
    along_bal = padded(canonical[2:4], (("bal", 0),), 1)
    outside = (along_space[0], along_space[3], along_bal[0], along_bal[3])
    summed = jnp.stack([canonical[side_index] + outside[side_index] for side_index in range(4)])
    return local_order(summed, inverse)


def local(panels, enrich, compliance, loads, face_maps, face_lengths, contact):
    panel_rows = panels[0, 0]
    columns = panel_rows.shape[1]
    face_len = columns // 4

    def add_block(block_number, running):
        block_data = lax.dynamic_slice_in_dim(panel_rows, block_number * BLOCK_ROWS, BLOCK_ROWS, 0)
        return running + lax.dot_general(
            block_data, block_data, (((0,), (0,)), ((), ())), preferred_element_type=jnp.float32
        )

    gram_matrix = lax.fori_loop(
        0, enrich[0, 0], add_block, jnp.zeros((columns, columns), jnp.float32)
    )
    diag_terms = compliance[0, 0]
    table = face_maps[0, 0]
    canon_slot = jnp.arange(face_len, dtype=jnp.int32)
    live_canon = (canon_slot[None, :] < face_lengths[0, 0][:, None]).astype(jnp.float32)
    inverse = jnp.argsort(table, axis=1)
    live_local = jnp.take_along_axis(live_canon, inverse, axis=1).reshape(1, columns)
    position = table + (jnp.arange(4, dtype=jnp.int32) * face_len)[:, None]
    center, half_span, ratio_c = chebyshev_constants()
    residual = assemble(live_local * loads[0, 0], position, inverse)
    direction = residual / center
    solution = jnp.zeros_like(residual)
    cheb_rho = 1.0 / ratio_c
    for iteration in range(ITERS):
        solution = solution + direction
        product = jnp.dot(direction, gram_matrix, precision=lax.Precision.HIGHEST)
        residual = residual - assemble(
            live_local * (product + direction * diag_terms[None, :]), position, inverse
        )
        if iteration + 1 < ITERS:
            rho_next = 1.0 / (2.0 * ratio_c - cheb_rho)
            direction = rho_next * cheb_rho * direction + 2.0 * rho_next / half_span * residual
            cheb_rho = rho_next
    gathered = jnp.take(solution, contact[0, 0], axis=1)
    negative = jnp.minimum(gathered, 0.0)
    own_terms = jnp.sum(negative * negative, axis=1)
    summed_terms = lax.psum(own_terms, ("space", "bal"))
    violation = jnp.sqrt(summed_terms + 1e-06)
    return (solution[None, None], residual[None, None], violation)


def solution(mesh):
    in_specs = (
        P("space", "bal", None, None),
        P("space", "bal"),
        P("space", "bal", None),
        P("space", "bal", None, None),
        P("space", "bal", None, None),
        P("space", "bal", None),
        P("space", "bal", None),
    )
    out_specs = (P("space", "bal", None, None), P("space", "bal", None, None), P())
    return jax.shard_map(local, mesh=mesh, in_specs=in_specs, out_specs=out_specs, check_vma=False)
```

profile of v0, /device:TPU:1, one launch (start us, length us, event | category | flops | bytes accessed | tf_op | source)
XLA Modules:
  0.0 281.4 jit_solution(9992371704102453064)
XLA Ops:
  9.4 2.5 broadcast_in_dim.44
  11.9 6.8 %while.10 = (s32[]{:T(128)}, f32[1024,1024]{1,0:T(8,128)}, s32[]{:T(128)}, bf16[1024,1024]{1,0:T(8,128)(2,1)S(1)}, s32[]{:T(128)}, /*index=5*/s32[]{:T(128)}, s32[]{:T(128)}, s32[]{:T(128)}) while((s32[]{:T(128)}, f32[1024,1024]{1,0:T(8,128)}, s32[]{:T(128)}, bf16[1024,1024]{1,0:T(8,128)(2,1)S(1)}, s32[]{:T(128)}, /*index=5*/s32[]{:T(128)}, ...), condition=%wide.region_2.5_spmd, body=%wide.region_1.4_spmd.sunk | while | flops 1074790400 | bytes 9437327 | solution.py:65
  12.6 5.4 %convolution_add_fusion.5 = f32[1024,1024]{1,0:T(8,128)} fusion(f32[1024,1024]{1,0:T(8,128)} %get-tuple-element.110, bf16[1024,1024]{1,0:T(8,128)(2,1)S(1)} %get-tuple-element.120, s32[]{:T(128)S(6)} %select_n.135), kind=kOutput, calls=%fused_computation.10.clone.1 | convolution fusion | flops 1074790400 | bytes 9437188 | tf_op jit(solution)/shard_map/while/body/dot_general | solution.py:61
  19.7 9.1 %gather_fusion.1 = f32[1024]{0:T(1024)S(1)} fusion(f32[4,256]{1,0:T(4,128)S(1)} %fusion.14, s32[1024]{0:T(1024)S(1)} %bitcast.134), kind=kCustom, calls=%fused_computation.9 | custom fusion | bytes 16384 | tf_op jit(solution)/shard_map/jit(take_along_axis)/gather | solution.py:73
  29.1 2.8 gather_fusion.2
  32.2 10.9 %collective-permute-start = (f32[1,64,256]{1,2,0:T(8,128)S(1)}, f32[1,64,256]{1,2,0:T(8,128)S(1)}, u32[]{:S(2)}, u32[]{:S(2)}) collective-permute-start(f32[1,64,256]{1,2,0:T(8,128)S(1)} %get-tuple-element.69), channel_id=1, source_target_pairs={{0,64},{64,128},{128,192},{192,256},{256,320},{320,384},{384,448},... | collective-permute-start | bytes 196616 | tf_op jit(solution)/shard_map/ppermute | solution.py:19
  46.4 8.2 %collective-permute-start.3 = (f32[1,64,256]{1,2,0:T(8,128)S(1)}, f32[1,64,256]{1,2,0:T(8,128)S(1)}, u32[]{:S(2)}, u32[]{:S(2)}) collective-permute-start(f32[1,64,256]{1,2,0:T(8,128)S(1)} %get-tuple-element.71), channel_id=1, source_target_pairs={{1,0},{2,1},{3,2},{4,3},{5,4},{6,5},{7,6},{8,7},{9,8},{10,9},{11,1... | collective-permute-start | bytes 196616 | tf_op jit(solution)/shard_map/ppermute | solution.py:22
  55.7 6.8 %gather_fusion.3 = f32[1024,64]{1,0:T(8,128)S(1)} fusion(f32[4,64,256]{1,2,0:T(8,128)S(1)} %pad_maximum_fusion, s32[1024]{0:T(1024)S(1)} %bitcast.130), kind=kCustom, calls=%fused_computation.1.clone | custom fusion | bytes 532480 | tf_op jit(solution)/shard_map/jit(take_along_axis)/gather | solution.py:41
  62.8 4.8 %fusion.4 = f32[64,1024]{1,0:T(8,128)S(1)} fusion(f32[1024,1024]{1,0:T(8,128)} %get-tuple-element.30, f32[64,1024]{1,0:T(8,128)S(1)} %bitcast.136, f32[1024]{0:T(1024)S(1)} %broadcast_multiply_fusion, f32[1024]{0:T(1024)S(1)} %bitcast.156), kind=kOutput, calls=%fused_computation.18 | convolution fusion | flops 805568512 | bytes 4726784 | tf_op jit(solution)/shard_map/dot_general | solution.py:82
  67.8 2.8 gather_fusion.4
  70.9 4.3 %collective-permute-start.4 = (f32[1,64,256]{1,2,0:T(8,128)S(1)}, f32[1,64,256]{1,2,0:T(8,128)S(1)}, u32[]{:S(2)}, u32[]{:S(2)}) collective-permute-start(f32[1,64,256]{1,2,0:T(8,128)S(1)} %get-tuple-element.61), channel_id=1, source_target_pairs={{0,64},{64,128},{128,192},{192,256},{256,320},{320,384},{384,448},... | collective-permute-start | bytes 196616 | tf_op jit(solution)/shard_map/ppermute | solution.py:19
  78.4 2.4 collective-permute-start.7
  81.9 2.8 collective-permute-done.7
  84.8 6.8 %gather_fusion.5 = f32[1024,64]{1,0:T(8,128)S(1)} fusion(f32[4,64,256]{1,2,0:T(8,128)S(1)} %pad_maximum_fusion.1, s32[1024]{0:T(1024)S(1)} %bitcast.131), kind=kCustom, calls=%fused_computation.5.clone | custom fusion | bytes 532480 | tf_op jit(solution)/shard_map/jit(take_along_axis)/gather | solution.py:41
  92.0 4.9 %fusion.3 = f32[64,1024]{1,0:T(8,128)S(1)} fusion(f32[1024,1024]{1,0:T(8,128)} %get-tuple-element.30, f32[1024]{0:T(1024)S(1)} %bitcast.160, f32[64,1024]{1,0:T(8,128)S(1)} %sub.48, f32[64,1024]{1,0:T(8,128)S(1)} %bitcast.138, f32[1024]{0:T(1024)S(1)} %bitcast.157), kind=kOutput, calls=%fused_computation.16 | convolution fusion | flops 805896192 | bytes 4988928 | tf_op jit(solution)/shard_map/dot_general | solution.py:82
  97.1 2.8 gather_fusion.6
  100.1 4.3 %collective-permute-start.8 = (f32[1,64,256]{1,2,0:T(8,128)S(1)}, f32[1,64,256]{1,2,0:T(8,128)S(1)}, u32[]{:S(2)}, u32[]{:S(2)}) collective-permute-start(f32[1,64,256]{1,2,0:T(8,128)S(1)} %get-tuple-element.53), channel_id=1, source_target_pairs={{0,64},{64,128},{128,192},{192,256},{256,320},{320,384},{384,448},... | collective-permute-start | bytes 196616 | tf_op jit(solution)/shard_map/ppermute | solution.py:19
  107.8 2.5 collective-permute-start.11
  114.2 6.8 %gather_fusion.7 = f32[1024,64]{1,0:T(8,128)S(1)} fusion(f32[4,64,256]{1,2,0:T(8,128)S(1)} %pad_maximum_fusion.2, s32[1024]{0:T(1024)S(1)} %bitcast.132), kind=kCustom, calls=%fused_computation.6.clone | custom fusion | bytes 532480 | tf_op jit(solution)/shard_map/jit(take_along_axis)/gather | solution.py:41
  121.6 4.9 %fusion.2 = f32[64,1024]{1,0:T(8,128)S(1)} fusion(f32[1024,1024]{1,0:T(8,128)} %get-tuple-element.30, f32[1024]{0:T(1024)S(1)} %bitcast.161, f32[64,1024]{1,0:T(8,128)S(1)} %sub.48, f32[64,1024]{1,0:T(8,128)S(1)} %bitcast.141, f32[64,1024]{1,0:T(8,128)S(1)} %bitcast.139, f32[1024]{0:T(1024)S(1)} %bitcast.158), kind=kOutput, calls=%fused_computation.14 | convolution fusion | flops 806420480 | bytes 5251072 | tf_op jit(solution)/shard_map/dot_general | solution.py:82
  126.8 2.8 gather_fusion.8
  129.9 5.6 %collective-permute-start.12 = (f32[1,64,256]{1,2,0:T(8,128)S(1)}, f32[1,64,256]{1,2,0:T(8,128)S(1)}, u32[]{:S(2)}, u32[]{:S(2)}) collective-permute-start(f32[1,64,256]{1,2,0:T(8,128)S(1)} %get-tuple-element.45), channel_id=1, source_target_pairs={{0,64},{64,128},{128,192},{192,256},{256,320},{320,384},{384,448},... | collective-permute-start | bytes 196616 | tf_op jit(solution)/shard_map/ppermute | solution.py:19
  142.1 122.9 %psum.7 = f32[64]{0:T(128)S(1)} all-reduce(f32[64]{0:T(128)S(1)} %multiply_reduce_fusion), channel_id=1, replica_groups=mesh['space'=12,'bal'=64] {'space','bal'}, use_global_device_ids=true, to_apply=%region_4.7 | all-reduce | flops 64 | bytes 512 | tf_op jit(solution)/shard_map/psum | solution.py:93
  266.5 6.8 %gather_fusion.9 = f32[1024,64]{1,0:T(8,128)S(1)} fusion(f32[4,64,256]{1,2,0:T(8,128)S(1)} %pad_maximum_fusion.3, s32[1024]{0:T(1024)S(1)} %bitcast.133), kind=kCustom, calls=%fused_computation.7.clone | custom fusion | bytes 532480 | tf_op jit(solution)/shard_map/jit(take_along_axis)/gather | solution.py:41
  (97 shorter events, 31.3 us)
Async XLA Ops:
  7.2 4.8 %copy-start = (bf16[1,1,1024,1024]{3,2,1,0:T(8,128)(2,1)S(1)}, bf16[1,1,1024,1024]{3,2,1,0:T(8,128)(2,1)}, u32[]{:S(2)}) copy-start(bf16[1,1,1024,1024]{3,2,1,0:T(8,128)(2,1)} %param.13) | copy-start | bytes 6291460
  7.2 11.7 %sort.19.cloned.1.call-start = ((), (), s32[]{:S(2)}) async-start(), calls=%async_computation | async-start | bytes 24608 | tf_op jit(solution)/shard_map/jit(argsort)/sort | solution.py:72
  11.9 6.8 %copy-start.4 = (s32[1,1,4]{2,1,0:T(1,128)S(1)}, s32[1,1,4]{2,1,0:T(1,128)}, u32[]{:S(2)}) copy-start(s32[1,1,4]{2,1,0:T(1,128)} %param.18) | copy-start | bytes 52
  11.9 6.9 %copy-start.2 = (f32[1,1,1024]{2,1,0:T(1,128)S(1)}, f32[1,1,1024]{2,1,0:T(1,128)}, u32[]{:S(2)}) copy-start(f32[1,1,1024]{2,1,0:T(1,128)} %param.15) | copy-start | bytes 12292
  11.9 6.9 %copy-start.5 = (s32[1,1,128]{2,1,0:T(1,128)S(1)}, s32[1,1,128]{2,1,0:T(1,128)}, u32[]{:S(2)}) copy-start(s32[1,1,128]{2,1,0:T(1,128)} %param.19) | copy-start | bytes 1540
  18.7 10.1 %copy-start.1 = (f32[1,1,64,1024]{3,2,1,0:T(8,128)S(1)}, f32[1,1,64,1024]{3,2,1,0:T(8,128)}, u32[]{:S(2)}) copy-start(f32[1,1,64,1024]{3,2,1,0:T(8,128)} %param.16) | copy-start | bytes 786436
  18.9 9.9 %copy-start.3 = (s32[4,256]{1,0:T(4,128)S(1)}, s32[4,256]{1,0:T(4,128)}, u32[]{:S(2)}) copy-start(s32[4,256]{1,0:T(4,128)} %get-tuple-element.29) | copy-start | bytes 12292
  32.2 22.4 %collective-permute-start = (f32[1,64,256]{1,2,0:T(8,128)S(1)}, f32[1,64,256]{1,2,0:T(8,128)S(1)}, u32[]{:S(2)}, u32[]{:S(2)}) collective-permute-start(f32[1,64,256]{1,2,0:T(8,128)S(1)} %get-tuple-element.69), channel_id=1, source_target_pairs={{0,64},{64,128},{128,192},{192,256},{256,320},{320,384},{384,448},... | collective-permute-start | bytes 196616 | tf_op jit(solution)/shard_map/ppermute | solution.py:19
  43.1 11.5 %collective-permute-start.1 = (f32[1,64,256]{1,2,0:T(8,128)S(1)}, f32[1,64,256]{1,2,0:T(8,128)S(1)}, u32[]{:S(2)}, u32[]{:S(2)}) collective-permute-start(f32[1,64,256]{1,2,0:T(8,128)S(1)} %get-tuple-element.72), channel_id=1, source_target_pairs={{64,0},{128,64},{192,128},{256,192},{320,256},{384,320},{448,384},... | collective-permute-start | bytes 196616 | tf_op jit(solution)/shard_map/ppermute | solution.py:22
  44.4 10.2 %collective-permute-start.2 = (f32[1,64,256]{1,2,0:T(8,128)S(1)}, f32[1,64,256]{1,2,0:T(8,128)S(1)}, u32[]{:S(2)}, u32[]{:S(2)}) collective-permute-start(f32[1,64,256]{1,2,0:T(8,128)S(1)} %get-tuple-element.70), channel_id=1, source_target_pairs={{0,1},{1,2},{2,3},{3,4},{4,5},{5,6},{6,7},{7,8},{8,9},{9,10},{10,1... | collective-permute-start | bytes 196616 | tf_op jit(solution)/shard_map/ppermute | solution.py:19
  46.4 9.2 %collective-permute-start.3 = (f32[1,64,256]{1,2,0:T(8,128)S(1)}, f32[1,64,256]{1,2,0:T(8,128)S(1)}, u32[]{:S(2)}, u32[]{:S(2)}) collective-permute-start(f32[1,64,256]{1,2,0:T(8,128)S(1)} %get-tuple-element.71), channel_id=1, source_target_pairs={{1,0},{2,1},{3,2},{4,3},{5,4},{6,5},{7,6},{8,7},{9,8},{10,9},{11,1... | collective-permute-start | bytes 196616 | tf_op jit(solution)/shard_map/ppermute | solution.py:22
  70.9 9.9 %collective-permute-start.4 = (f32[1,64,256]{1,2,0:T(8,128)S(1)}, f32[1,64,256]{1,2,0:T(8,128)S(1)}, u32[]{:S(2)}, u32[]{:S(2)}) collective-permute-start(f32[1,64,256]{1,2,0:T(8,128)S(1)} %get-tuple-element.61), channel_id=1, source_target_pairs={{0,64},{64,128},{128,192},{192,256},{256,320},{320,384},{384,448},... | collective-permute-start | bytes 196616 | tf_op jit(solution)/shard_map/ppermute | solution.py:19
  75.2 6.7 %collective-permute-start.5 = (f32[1,64,256]{1,2,0:T(8,128)S(1)}, f32[1,64,256]{1,2,0:T(8,128)S(1)}, u32[]{:S(2)}, u32[]{:S(2)}) collective-permute-start(f32[1,64,256]{1,2,0:T(8,128)S(1)} %get-tuple-element.64), channel_id=1, source_target_pairs={{64,0},{128,64},{192,128},{256,192},{320,256},{384,320},{448,384},... | collective-permute-start | bytes 196616 | tf_op jit(solution)/shard_map/ppermute | solution.py:22
  76.5 5.4 %collective-permute-start.6 = (f32[1,64,256]{1,2,0:T(8,128)S(1)}, f32[1,64,256]{1,2,0:T(8,128)S(1)}, u32[]{:S(2)}, u32[]{:S(2)}) collective-permute-start(f32[1,64,256]{1,2,0:T(8,128)S(1)} %get-tuple-element.62), channel_id=1, source_target_pairs={{0,1},{1,2},{2,3},{3,4},{4,5},{5,6},{6,7},{7,8},{8,9},{9,10},{10,1... | collective-permute-start | bytes 196616 | tf_op jit(solution)/shard_map/ppermute | solution.py:19
  78.4 6.3 %collective-permute-start.7 = (f32[1,64,256]{1,2,0:T(8,128)S(1)}, f32[1,64,256]{1,2,0:T(8,128)S(1)}, u32[]{:S(2)}, u32[]{:S(2)}) collective-permute-start(f32[1,64,256]{1,2,0:T(8,128)S(1)} %get-tuple-element.63), channel_id=1, source_target_pairs={{1,0},{2,1},{3,2},{4,3},{5,4},{6,5},{7,6},{8,7},{9,8},{10,9},{11,1... | collective-permute-start | bytes 196616 | tf_op jit(solution)/shard_map/ppermute | solution.py:22
  100.1 10.2 %collective-permute-start.8 = (f32[1,64,256]{1,2,0:T(8,128)S(1)}, f32[1,64,256]{1,2,0:T(8,128)S(1)}, u32[]{:S(2)}, u32[]{:S(2)}) collective-permute-start(f32[1,64,256]{1,2,0:T(8,128)S(1)} %get-tuple-element.53), channel_id=1, source_target_pairs={{0,64},{64,128},{128,192},{192,256},{256,320},{320,384},{384,448},... | collective-permute-start | bytes 196616 | tf_op jit(solution)/shard_map/ppermute | solution.py:19
  104.5 7.4 %collective-permute-start.9 = (f32[1,64,256]{1,2,0:T(8,128)S(1)}, f32[1,64,256]{1,2,0:T(8,128)S(1)}, u32[]{:S(2)}, u32[]{:S(2)}) collective-permute-start(f32[1,64,256]{1,2,0:T(8,128)S(1)} %get-tuple-element.56), channel_id=1, source_target_pairs={{64,0},{128,64},{192,128},{256,192},{320,256},{384,320},{448,384},... | collective-permute-start | bytes 196616 | tf_op jit(solution)/shard_map/ppermute | solution.py:22
  105.8 6.1 %collective-permute-start.10 = (f32[1,64,256]{1,2,0:T(8,128)S(1)}, f32[1,64,256]{1,2,0:T(8,128)S(1)}, u32[]{:S(2)}, u32[]{:S(2)}) collective-permute-start(f32[1,64,256]{1,2,0:T(8,128)S(1)} %get-tuple-element.54), channel_id=1, source_target_pairs={{0,1},{1,2},{2,3},{3,4},{4,5},{5,6},{6,7},{7,8},{8,9},{9,10},{10,1... | collective-permute-start | bytes 196616 | tf_op jit(solution)/shard_map/ppermute | solution.py:19
  107.8 6.3 %collective-permute-start.11 = (f32[1,64,256]{1,2,0:T(8,128)S(1)}, f32[1,64,256]{1,2,0:T(8,128)S(1)}, u32[]{:S(2)}, u32[]{:S(2)}) collective-permute-start(f32[1,64,256]{1,2,0:T(8,128)S(1)} %get-tuple-element.55), channel_id=1, source_target_pairs={{1,0},{2,1},{3,2},{4,3},{5,4},{6,5},{7,6},{8,7},{9,8},{10,9},{11,1... | collective-permute-start | bytes 196616 | tf_op jit(solution)/shard_map/ppermute | solution.py:22
  129.9 136.5 %collective-permute-start.12 = (f32[1,64,256]{1,2,0:T(8,128)S(1)}, f32[1,64,256]{1,2,0:T(8,128)S(1)}, u32[]{:S(2)}, u32[]{:S(2)}) collective-permute-start(f32[1,64,256]{1,2,0:T(8,128)S(1)} %get-tuple-element.45), channel_id=1, source_target_pairs={{0,64},{64,128},{128,192},{192,256},{256,320},{320,384},{384,448},... | collective-permute-start | bytes 196616 | tf_op jit(solution)/shard_map/ppermute | solution.py:19
  135.5 130.9 %collective-permute-start.13 = (f32[1,64,256]{1,2,0:T(8,128)S(1)}, f32[1,64,256]{1,2,0:T(8,128)S(1)}, u32[]{:S(2)}, u32[]{:S(2)}) collective-permute-start(f32[1,64,256]{1,2,0:T(8,128)S(1)} %get-tuple-element.48), channel_id=1, source_target_pairs={{64,0},{128,64},{192,128},{256,192},{320,256},{384,320},{448,384},... | collective-permute-start | bytes 196616 | tf_op jit(solution)/shard_map/ppermute | solution.py:22
  136.8 129.6 %collective-permute-start.14 = (f32[1,64,256]{1,2,0:T(8,128)S(1)}, f32[1,64,256]{1,2,0:T(8,128)S(1)}, u32[]{:S(2)}, u32[]{:S(2)}) collective-permute-start(f32[1,64,256]{1,2,0:T(8,128)S(1)} %get-tuple-element.46), channel_id=1, source_target_pairs={{0,1},{1,2},{2,3},{3,4},{4,5},{5,6},{6,7},{7,8},{8,9},{9,10},{10,1... | collective-permute-start | bytes 196616 | tf_op jit(solution)/shard_map/ppermute | solution.py:19
  138.9 127.5 %collective-permute-start.15 = (f32[1,64,256]{1,2,0:T(8,128)S(1)}, f32[1,64,256]{1,2,0:T(8,128)S(1)}, u32[]{:S(2)}, u32[]{:S(2)}) collective-permute-start(f32[1,64,256]{1,2,0:T(8,128)S(1)} %get-tuple-element.47), channel_id=1, source_target_pairs={{1,0},{2,1},{3,2},{4,3},{5,4},{6,5},{7,6},{8,7},{9,8},{10,9},{11,1... | collective-permute-start | bytes 196616 | tf_op jit(solution)/shard_map/ppermute | solution.py:22
Sparse Core Ops, SparseCore 0:
  10.9 2.5 sort.21.cloned.1.call-done
  (1 shorter events, 0.0 us)
where the time goes:
time: 283 us; the launch traced here: 281 us
  blocking collectives  123 us (43%)
  local copies, waits for them, and re-layouts  55.2 us (20%)
  starting transfers between devices  53.7 us (19%)
  matrix products  20 us (7%)
  between operations  14.7 us (5%)
  waiting for transfers between devices  8.58 us (3%)
  other arithmetic  4.91 us (2%)
    psum x1, blocking collectives, local(): summed_terms = lax.psum(own_terms, ('space', 'bal'))  123 us
    ppermute x8, starting transfers between devices, padded(): lax.ppermute(lax.slice_in_dim(block, block.shape[dim] - width, None, axis...  33.2 us
    gather x8, local copies, waits for them, and re-layouts, local_order(): face_rows = jnp.take_along_axis(summed, inverse[:, None, :], axis=2)  28 us
    ppermute x8, starting transfers between devices, padded(): lax.ppermute(lax.slice_in_dim(block, 0, width, axis=dim), axis, backward)  20.5 us
    dot_general x3, matrix products, local(): product = jnp.dot(direction, gram_matrix, precision=lax.Precision.HIGHEST)  14.6 us
    gather x4, local copies, waits for them, and re-layouts, canon_order(): picked = jnp.take(field, position, axis=1)  11.2 us
    gather x2, local copies, waits for them, and re-layouts, local(): jnp.take_along_axis(live_canon, inverse, axis=1).reshape(1, columns)  9.15 us
    ppermute x8, waiting for transfers between devices, padded(): lax.ppermute(lax.slice_in_dim(block, 0, width, axis=dim), axis, backward)  8.55 us
  transfers between devices with their start and end apart: 16, of which 5 were waited for; matrix products, arithmetic and copies ran while one was open for 1% of the time, Pallas kernels for 0%

commit v1 on v0

v1 whole, which is shorter than its diff:
```python
import functools
import math

import jax
import jax.numpy as jnp
from jax import lax
from jax.experimental import pallas as pl
from jax.experimental.pallas import tpu as pltpu
from jax.sharding import PartitionSpec as P

IFACE = 1024
FACE = 256
ROWS = 1024
BLOCK_ROWS = 512
LOADS = 64
ITERS = 3
CONTACT = 128
F32 = jnp.float32
BF16 = jnp.bfloat16
VM = pl.BlockSpec(memory_space=pltpu.VMEM)
SM = pl.BlockSpec(memory_space=pltpu.SMEM)
NN = (((1,), (0,)), ((), ()))
NT = (((1,), (1,)), ((), ()))


def chebyshev_constants():
    upper = 2.6 * (1.0 + math.sqrt(IFACE / ROWS)) ** 2 + 4.0
    lower = 0.5
    center = (upper + lower) / 2.0
    half_span = (upper - lower) / 2.0
    return (center, half_span, center / half_span)


def pieces(value, count):
    out = []
    for _ in range(count):
        piece = value.astype(BF16)
        out.append(piece)
        value = value - piece.astype(F32)
    return jnp.concatenate(out, axis=0)


def stacked_dot(value, matrix, dims, count):
    rows = value.shape[0]
    prod = lax.dot_general(pieces(value, count), matrix, dims, preferred_element_type=F32)
    total = prod[(count - 1) * rows :]
    for index in range(count - 2, -1, -1):
        total = total + prod[index * rows : (index + 1) * rows]
    return total


def one_hot(table_row):
    row = lax.broadcasted_iota(jnp.int32, (FACE, FACE), 0)
    return (row == table_row).astype(F32).astype(BF16)


def live_slots(lengths, face):
    slot = lax.broadcasted_iota(jnp.int32, (1, FACE), 1)
    return (slot < lengths[0, face]).astype(F32)


def loads_kernel(lengths, table, loads, perm, *sends):
    for face in range(4):
        hot = one_hot(table[face : face + 1, :])
        perm[face] = hot
        part = loads[:, face * FACE : (face + 1) * FACE]
        sends[face][...] = stacked_dot(part, hot, NN, 3) * live_slots(lengths, face)


def panel_kernel(enrich, panel, perm, compliance, contact, kept, diag, counts):
    live_rows = enrich[0, 0] * BLOCK_ROWS
    keep = lax.broadcasted_iota(jnp.int32, (ROWS, FACE), 0) < live_rows
    across = jnp.broadcast_to(contact[...], (CONTACT, CONTACT)).T
    for face in range(4):
        cols = slice(face * FACE, (face + 1) * FACE)
        moved = lax.dot_general(panel[:, cols], perm[face], NN, preferred_element_type=F32)
        kept[:, cols] = jnp.where(keep, moved, 0.0).astype(BF16)
        part = jnp.broadcast_to(compliance[:, cols], (8, FACE))
        diag[:, cols] = stacked_dot(part, perm[face], NN, 3)[0:1]
        tallies = []
        for half in range(FACE // CONTACT):
            base = face * FACE + half * CONTACT
            index = lax.broadcasted_iota(jnp.int32, (CONTACT, CONTACT), 1) + base
            tallies.append(jnp.sum((across == index).astype(F32), axis=0, keepdims=True))
        tally = jnp.broadcast_to(jnp.concatenate(tallies, axis=1), (8, FACE)).astype(BF16)
        counts[:, cols] = lax.dot_general(tally, perm[face], NN, preferred_element_type=F32)[0:1]


def step_kernel(first, last, keep_dir, add_res, lengths, kept, diag, *refs):
    own, got = refs[0:4], refs[4:8]
    refs = refs[8:]
    assembled = jnp.concatenate([o[...] + g[...] for o, g in zip(own, got)], axis=1)
    if first:
        residual = assembled
        direction = residual * add_res
        solution = direction
    else:
        residual = refs[0][...] - assembled
        direction = keep_dir * refs[1][...] + add_res * residual
        solution = refs[2][...] + direction
        refs = refs[3:]
    if last:
        counts, refs = refs[0], refs[1:]
    out_res, out_dir, out_sol = refs[0:3]
    sends = refs[3:7]
    out_res[...] = residual
    out_dir[...] = direction
    out_sol[...] = solution
    projected = stacked_dot(direction, kept[...], NT, 2)
    image = stacked_dot(projected, kept[...], NN, 2) + direction * diag[...]
    for face in range(4):
        cols = slice(face * FACE, (face + 1) * FACE)
        sends[face][...] = image[:, cols] * live_slots(lengths, face)
    if last:
        negative = jnp.minimum(solution, 0.0)
        weights = jnp.broadcast_to(counts[...], (8, IFACE)).astype(BF16)
        square = negative * negative
        terms = jnp.zeros((8, LOADS), F32)
        for _ in range(3):
            piece = square.astype(BF16)
            square = square - piece.astype(F32)
            terms = terms + lax.dot_general(weights, piece, NT, preferred_element_type=F32)
        refs[7][...] = jnp.broadcast_to(terms[0:1], refs[7].shape)


def solution_kernel(perm, field, out):
    for face in range(4):
        cols = slice(face * FACE, (face + 1) * FACE)
        out[:, cols] = stacked_dot(field[:, cols], perm[face], NT, 3)


def residual_kernel(perm, field, *refs):
    own, got, out = refs[0:4], refs[4:8], refs[8]
    for face in range(4):
        cols = slice(face * FACE, (face + 1) * FACE)
        value = field[:, cols] - (own[face][...] + got[face][...])
        out[:, cols] = stacked_dot(value, perm[face], NT, 3)


def call(body, name, out_shapes, in_specs):
    return pl.pallas_call(
        body,
        name=name,
        out_shape=[jax.ShapeDtypeStruct(shape, dtype) for shape, dtype in out_shapes],
        in_specs=in_specs,
        out_specs=[VM] * len(out_shapes),
    )


def exchange(sends):
    got = [None] * 4
    for axis, low in (("space", 0), ("bal", 2)):
        count = lax.axis_size(axis)
        forward = [(i, i + 1) for i in range(count - 1)]
        backward = [(target, source) for source, target in forward]
        got[low] = lax.ppermute(sends[low + 1], axis, forward)
        got[low + 1] = lax.ppermute(sends[low], axis, backward)
    return got


def total_over(row, axis):
    count = lax.axis_size(axis)
    spread = jnp.broadcast_to(row[None, :], (count, row.shape[0]))
    return jnp.sum(lax.all_to_all(spread, axis, 0, 0), axis=0)


def local(panels, enrich, compliance, loads, face_maps, face_lengths, contact):
    lengths = face_lengths.reshape(1, 4)
    center, half_span, ratio = chebyshev_constants()
    face_field = ((LOADS, FACE), F32)
    field = ((LOADS, IFACE), F32)
    perm, *sends = call(
        loads_kernel, "loads", [((4, FACE, FACE), BF16)] + [face_field] * 4, [SM, VM, VM]
    )(lengths, face_maps[0, 0], loads[0, 0])
    got = exchange(sends)
    kept, diag, counts = call(
        panel_kernel,
        "panel",
        [((ROWS, IFACE), BF16), ((1, IFACE), F32), ((1, IFACE), F32)],
        [SM, VM, VM, VM, VM],
    )(enrich, panels[0, 0], perm, compliance[0], contact[0])
    state = []
    rho = 1.0 / ratio
    keep_dir, add_res = 0.0, 1.0 / center
    for iteration in range(ITERS):
        last = iteration + 1 == ITERS
        inputs = [lengths, kept, diag, *sends, *got, *state] + ([counts] if last else [])
        outs = call(
            functools.partial(step_kernel, iteration == 0, last, keep_dir, add_res),
            "step",
            [field] * 3 + [face_field] * 4 + ([((8, LOADS), F32)] if last else []),
            [SM] + [VM] * (len(inputs) - 1),
        )(*inputs)
        state, sends = outs[0:3], outs[3:7]
        got = exchange(sends)
        rho_next = 1.0 / (2.0 * ratio - rho)
        keep_dir, add_res = rho_next * rho, 2.0 * rho_next / half_span
        rho = rho_next
    terms = outs[7][0]
    (solved,) = call(solution_kernel, "solved", [field], [VM, VM])(perm, state[2])
    (residual,) = call(residual_kernel, "residual", [field], [VM] * 10)(
        perm, state[0], *sends, *got
    )
    violation = jnp.sqrt(total_over(total_over(terms, "bal"), "space") + 1e-06)
    return (solved[None, None], residual[None, None], violation)


def solution(mesh):
    in_specs = (
        P("space", "bal", None, None),
        P("space", "bal"),
        P("space", "bal", None),
        P("space", "bal", None, None),
        P("space", "bal", None, None),
        P("space", "bal", None),
        P("space", "bal", None),
    )
    out_specs = (P("space", "bal", None, None), P("space", "bal", None, None), P())
    return jax.shard_map(local, mesh=mesh, in_specs=in_specs, out_specs=out_specs, check_vma=False)
```

time: 283 us -> 123 us (0.43)
  the two profiles are of different devices: /device:TPU:1 before, /device:TPU:2 now
where the time goes in v1:
time: 123 us; the launch traced here: 122 us
  starting transfers between devices  63.1 us (51%)
  Pallas kernels  21.8 us (18%)
  waiting for transfers between devices  17.5 us (14%)
  blocking collectives  13.9 us (11%)
  local copies, waits for them, and re-layouts  3.76 us (3%)
  between operations  1.6 us (1%)
    ppermute x8, starting transfers between devices, exchange(): got[low] = lax.ppermute(sends[low + 1], axis, forward)  27.9 us
    ppermute x8, starting transfers between devices, exchange(): got[low + 1] = lax.ppermute(sends[low], axis, backward)  17.8 us
    all_to_all x1, starting transfers between devices, total_over(): return jnp.sum(lax.all_to_all(spread, axis, 0, 0), axis=0)  17.4 us
    ppermute x8, waiting for transfers between devices, exchange(): got[low] = lax.ppermute(sends[low + 1], axis, forward)  17.3 us
    all_to_all x1, blocking collectives, total_over(): return jnp.sum(lax.all_to_all(spread, axis, 0, 0), axis=0)  13.9 us
    pallas_call x3, Pallas kernels, local(): call(functools.partial(step_kernel, iteration == 0, last, keep_dir, add_r...  11.3 us
    pallas_call x1, Pallas kernels, local(): call(panel_kernel, 'panel', [((ROWS, IFACE), BF16), ((1, IFACE), F32), ((...  4.04 us
    unnamed x32, local copies, waits for them, and re-layouts  2.47 us
  transfers between devices with their start and end apart: 17, of which 5 were waited for; matrix products, arithmetic and copies ran while one was open for 0% of the time, Pallas kernels for 5%

profile of v1, /device:TPU:2, one launch (start us, length us, event | category | flops | bytes accessed | tf_op | source)
XLA Modules:
  0.0 122.2 jit_solution(4660088082568287471)
XLA Ops:
  0.6 2.0 %loads.1 = (bf16[4,256,256]{2,1,0:T(8,128)(2,1)}, f32[64,256]{1,0:T(8,128)}, f32[64,256]{1,0:T(8,128)}, f32[64,256]{1,0:T(8,128)}, f32[64,256]{1,0:T(8,128)}) custom-call(s32[1,4]{1,0:T(1,128)} %bitcast.16, s32[4,256]{1,0:T(4,128)} %bitcast.20, f32[64,1024]{1,0:T(8,128)} %bitcast.12), custom_call_target="tpu_custom_call" | custom-call | tf_op jit(solution)/shard_map/loads/pallas_call | solution.py:172
  3.9 4.9 %collective-permute-start = (f32[64,256]{1,0:T(8,128)}, f32[64,256]{1,0:T(8,128)S(1)}, u32[]{:S(2)}, u32[]{:S(2)}) collective-permute-start(f32[64,256]{1,0:T(8,128)} %get-tuple-element.36.refs_1_), channel_id=1, source_target_pairs={{0,64},{64,128},{128,192},{192,256},{256,320},{320,384},{384,448},... | collective-permute-start | bytes 196616 | tf_op jit(solution)/shard_map/ppermute | solution.py:156
  8.8 4.5 %collective-permute-start.3 = (f32[64,256]{1,0:T(8,128)}, f32[64,256]{1,0:T(8,128)S(1)}, u32[]{:S(2)}, u32[]{:S(2)}) collective-permute-start(f32[64,256]{1,0:T(8,128)} %get-tuple-element.37.refs_2_), channel_id=1, source_target_pairs={{1,0},{2,1},{3,2},{4,3},{5,4},{6,5},{7,6},{8,7},{9,8},{10,9},{11,1... | collective-permute-start | bytes 196616 | tf_op jit(solution)/shard_map/ppermute | solution.py:157
  13.4 1.9 %collective-permute-start.2 = (f32[64,256]{1,0:T(8,128)}, f32[64,256]{1,0:T(8,128)S(1)}, u32[]{:S(2)}, u32[]{:S(2)}) collective-permute-start(f32[64,256]{1,0:T(8,128)} %get-tuple-element.38.refs_3_), channel_id=1, source_target_pairs={{0,1},{1,2},{2,3},{3,4},{4,5},{5,6},{6,7},{7,8},{8,9},{9,10},{10,1... | collective-permute-start | bytes 196616 | tf_op jit(solution)/shard_map/ppermute | solution.py:156
  15.9 4.0 %panel.1 = (bf16[1024,1024]{1,0:T(8,128)(2,1)}, f32[1,1024]{1,0:T(1,128)}, f32[1,1024]{1,0:T(1,128)}) custom-call(s32[1,1]{1,0:T(1,128)S(6)} %copy.11.enrich, bf16[1024,1024]{1,0:T(8,128)(2,1)} %bitcast.11, bf16[4,256,256]{2,1,0:T(8,128)(2,1)} %get-tuple-element.32.perm, f32[1,1024]{1,0:T(1,128)} %bitcast.21, s32[1,128]{1,0:T(1,128)} %bitcast.22), custom_call_target="tpu_custom_call" | custom-call | tf_op jit(solution)/shard_map/panel/pallas_call | solution.py:176
  21.9 3.6 %step.3 = (f32[64,1024]{1,0:T(8,128)}, f32[64,1024]{1,0:T(8,128)}, f32[64,1024]{1,0:T(8,128)}, f32[64,256]{1,0:T(8,128)}, f32[64,256]{1,0:T(8,128)}, /*index=5*/f32[64,256]{1,0:T(8,128)}, f32[64,256]{1,0:T(8,128)}) custom-call(s32[1,4]{1,0:T(1,128)} %bitcast.17, bf16[1024,1024]{1,0:T(8,128)(2,1)} %get-tuple-element.33.kept, ...), custom_call_target="tpu_custom_call" | custom-call | tf_op jit(solution)/shard_map/step/pallas_call | solution.py:188
  26.8 4.9 %collective-permute-start.4 = (f32[64,256]{1,0:T(8,128)}, f32[64,256]{1,0:T(8,128)S(1)}, u32[]{:S(2)}, u32[]{:S(2)}) collective-permute-start(f32[64,256]{1,0:T(8,128)} %get-tuple-element.40.refs_1_), channel_id=1, source_target_pairs={{0,64},{64,128},{128,192},{192,256},{256,320},{320,384},{384,448},... | collective-permute-start | bytes 196616 | tf_op jit(solution)/shard_map/ppermute | solution.py:156
  31.7 4.3 %collective-permute-start.7 = (f32[64,256]{1,0:T(8,128)}, f32[64,256]{1,0:T(8,128)S(1)}, u32[]{:S(2)}, u32[]{:S(2)}) collective-permute-start(f32[64,256]{1,0:T(8,128)} %get-tuple-element.41.refs_2_), channel_id=1, source_target_pairs={{1,0},{2,1},{3,2},{4,3},{5,4},{6,5},{7,6},{8,7},{9,8},{10,9},{11,1... | collective-permute-start | bytes 196616 | tf_op jit(solution)/shard_map/ppermute | solution.py:157
  36.0 1.9 %collective-permute-start.6 = (f32[64,256]{1,0:T(8,128)}, f32[64,256]{1,0:T(8,128)S(1)}, u32[]{:S(2)}, u32[]{:S(2)}) collective-permute-start(f32[64,256]{1,0:T(8,128)} %get-tuple-element.42.refs_3_), channel_id=1, source_target_pairs={{0,1},{1,2},{2,3},{3,4},{4,5},{5,6},{6,7},{7,8},{8,9},{9,10},{10,1... | collective-permute-start | bytes 196616 | tf_op jit(solution)/shard_map/ppermute | solution.py:156
  38.2 5.7 %collective-permute-done.6.refs_6_ = f32[64,256]{1,0:T(8,128)S(1)} collective-permute-done((f32[64,256]{1,0:T(8,128)}, f32[64,256]{1,0:T(8,128)S(1)}, u32[]{:S(2)}, u32[]{:S(2)}) %collective-permute-start.6) | collective-permute-done | bytes 65568 | tf_op jit(solution)/shard_map/ppermute | solution.py:156
  44.5 3.8 %step.4 = (f32[64,1024]{1,0:T(8,128)}, f32[64,1024]{1,0:T(8,128)}, f32[64,1024]{1,0:T(8,128)}, f32[64,256]{1,0:T(8,128)}, f32[64,256]{1,0:T(8,128)}, /*index=5*/f32[64,256]{1,0:T(8,128)}, f32[64,256]{1,0:T(8,128)}) custom-call(s32[1,4]{1,0:T(1,128)} %bitcast.18, bf16[1024,1024]{1,0:T(8,128)(2,1)} %get-tuple-element.33.kept, ...), custom_call_target="tpu_custom_call" | custom-call | tf_op jit(solution)/shard_map/step/pallas_call | solution.py:188
  49.6 4.9 %collective-permute-start.8 = (f32[64,256]{1,0:T(8,128)}, f32[64,256]{1,0:T(8,128)S(1)}, u32[]{:S(2)}, u32[]{:S(2)}) collective-permute-start(f32[64,256]{1,0:T(8,128)} %get-tuple-element.47.refs_1_), channel_id=1, source_target_pairs={{0,64},{64,128},{128,192},{192,256},{256,320},{320,384},{384,448},... | collective-permute-start | bytes 196616 | tf_op jit(solution)/shard_map/ppermute | solution.py:156
  54.5 1.9 %collective-permute-start.11 = (f32[64,256]{1,0:T(8,128)}, f32[64,256]{1,0:T(8,128)S(1)}, u32[]{:S(2)}, u32[]{:S(2)}) collective-permute-start(f32[64,256]{1,0:T(8,128)} %get-tuple-element.48.refs_2_), channel_id=1, source_target_pairs={{1,0},{2,1},{3,2},{4,3},{5,4},{6,5},{7,6},{8,7},{9,8},{10,9},{11,1... | collective-permute-start | bytes 196616 | tf_op jit(solution)/shard_map/ppermute | solution.py:157
  56.4 2.4 %collective-permute-start.10 = (f32[64,256]{1,0:T(8,128)}, f32[64,256]{1,0:T(8,128)S(1)}, u32[]{:S(2)}, u32[]{:S(2)}) collective-permute-start(f32[64,256]{1,0:T(8,128)} %get-tuple-element.49.refs_3_), channel_id=1, source_target_pairs={{0,1},{1,2},{2,3},{3,4},{4,5},{5,6},{6,7},{7,8},{8,9},{9,10},{10,1... | collective-permute-start | bytes 196616 | tf_op jit(solution)/shard_map/ppermute | solution.py:156
  58.9 5.4 %collective-permute-done.10.refs_6_ = f32[64,256]{1,0:T(8,128)S(1)} collective-permute-done((f32[64,256]{1,0:T(8,128)}, f32[64,256]{1,0:T(8,128)S(1)}, u32[]{:S(2)}, u32[]{:S(2)}) %collective-permute-start.10) | collective-permute-done | bytes 65568 | tf_op jit(solution)/shard_map/ppermute | solution.py:156
  64.9 3.9 %step.5 = (f32[64,1024]{1,0:T(8,128)}, f32[64,1024]{1,0:T(8,128)}, f32[64,1024]{1,0:T(8,128)}, f32[64,256]{1,0:T(8,128)}, f32[64,256]{1,0:T(8,128)}, /*index=5*/...) custom-call(s32[1,4]{1,0:T(1,128)} %bitcast.19, bf16[1024,1024]{1,0:T(8,128)(2,1)} %get-tuple-element.33.kept, ...), custom_call_target="tpu_custom_call" | custom-call | tf_op jit(solution)/shard_map/step/pallas_call | solution.py:188
  69.6 13.9 %all_to_all.12 = f32[64,1,64]{2,1,0:T(1,128)S(1)} all-to-all(f32[64,1,64]{2,1,0:T(1,128)S(1)} %broadcast_in_dim.19), channel_id=1, replica_groups=mesh['space'=12,'bal'=64] {'bal'}, dimensions={0} | all-to-all | bytes 32768 | tf_op jit(solution)/shard_map/all_to_all | solution.py:164
  84.0 17.4 %all-to-all-start.1 = ((f32[12,1,64]{2,1,0:T(1,128)}), f32[12,1,64]{2,1,0:T(1,128)S(1)}, u32[]{:S(2)}, u32[]{:S(2)}) async-start(f32[12,1,64]{2,1,0:T(1,128)} %broadcast_in_dim.20), calls=%async_computation.1 | async-start | bytes 12288 | tf_op jit(solution)/shard_map/all_to_all | solution.py:164
  101.4 2.1 %solved.1 = f32[64,1024]{1,0:T(8,128)} custom-call(bf16[4,256,256]{2,1,0:T(8,128)(2,1)} %get-tuple-element.32.perm, f32[64,1024]{1,0:T(8,128)} %get-tuple-element.54.field), custom_call_target="tpu_custom_call" | custom-call | tf_op jit(solution)/shard_map/solved/pallas_call | solution.py:200
  104.9 4.5 %collective-permute-start.12 = (f32[64,256]{1,0:T(8,128)}, f32[64,256]{1,0:T(8,128)S(1)}, u32[]{:S(2)}, u32[]{:S(2)}) collective-permute-start(f32[64,256]{1,0:T(8,128)} %get-tuple-element.57.refs_1_), channel_id=1, source_target_pairs={{0,64},{64,128},{128,192},{192,256},{256,320},{320,384},{384,448},... | collective-permute-start | bytes 196616 | tf_op jit(solution)/shard_map/ppermute | solution.py:156
  109.4 1.9 %collective-permute-start.15 = (f32[64,256]{1,0:T(8,128)}, f32[64,256]{1,0:T(8,128)S(1)}, u32[]{:S(2)}, u32[]{:S(2)}) collective-permute-start(f32[64,256]{1,0:T(8,128)} %get-tuple-element.58.refs_2_), channel_id=1, source_target_pairs={{1,0},{2,1},{3,2},{4,3},{5,4},{6,5},{7,6},{8,7},{9,8},{10,9},{11,1... | collective-permute-start | bytes 196616 | tf_op jit(solution)/shard_map/ppermute | solution.py:157
  111.4 2.4 %collective-permute-start.14 = (f32[64,256]{1,0:T(8,128)}, f32[64,256]{1,0:T(8,128)S(1)}, u32[]{:S(2)}, u32[]{:S(2)}) collective-permute-start(f32[64,256]{1,0:T(8,128)} %get-tuple-element.59.refs_3_), channel_id=1, source_target_pairs={{0,1},{1,2},{2,3},{3,4},{4,5},{5,6},{6,7},{7,8},{8,9},{9,10},{10,1... | collective-permute-start | bytes 196616 | tf_op jit(solution)/shard_map/ppermute | solution.py:156
  114.4 4.9 %collective-permute-done.14.refs_6_ = f32[64,256]{1,0:T(8,128)S(1)} collective-permute-done((f32[64,256]{1,0:T(8,128)}, f32[64,256]{1,0:T(8,128)S(1)}, u32[]{:S(2)}, u32[]{:S(2)}) %collective-permute-start.14) | collective-permute-done | bytes 65568 | tf_op jit(solution)/shard_map/ppermute | solution.py:156
  119.9 2.3 %residual.1 = f32[64,1024]{1,0:T(8,128)} custom-call(bf16[4,256,256]{2,1,0:T(8,128)(2,1)} %get-tuple-element.32.perm, f32[64,1024]{1,0:T(8,128)} %get-tuple-element.55.field, f32[64,256]{1,0:T(8,128)} %get-tuple-element.56.refs_0_, f32[64,256]{1,0:T(8,128)} %get-tuple-element.57.refs_1_, f32[64,256]{1,0:T(8,128)} %get-tuple-element.58.refs_2_, ...), custom_call_target="tpu_custom_call" | custom-call | tf_op jit(solution)/shard_map/residual/pallas_call | solution.py:201
  (56 shorter events, 11.0 us)
Async XLA Ops:
  2.6 17.3 %collective-permute-start.1 = (f32[64,256]{1,0:T(8,128)}, f32[64,256]{1,0:T(8,128)S(1)}, u32[]{:S(2)}, u32[]{:S(2)}) collective-permute-start(f32[64,256]{1,0:T(8,128)} %get-tuple-element.35.refs_0_), channel_id=1, source_target_pairs={{64,0},{128,64},{192,128},{256,192},{320,256},{384,320},{448,384},... | collective-permute-start | bytes 196616 | tf_op jit(solution)/shard_map/ppermute | solution.py:157
  3.9 16.1 %collective-permute-start = (f32[64,256]{1,0:T(8,128)}, f32[64,256]{1,0:T(8,128)S(1)}, u32[]{:S(2)}, u32[]{:S(2)}) collective-permute-start(f32[64,256]{1,0:T(8,128)} %get-tuple-element.36.refs_1_), channel_id=1, source_target_pairs={{0,64},{64,128},{128,192},{192,256},{256,320},{320,384},{384,448},... | collective-permute-start | bytes 196616 | tf_op jit(solution)/shard_map/ppermute | solution.py:156
  8.8 11.2 %collective-permute-start.3 = (f32[64,256]{1,0:T(8,128)}, f32[64,256]{1,0:T(8,128)S(1)}, u32[]{:S(2)}, u32[]{:S(2)}) collective-permute-start(f32[64,256]{1,0:T(8,128)} %get-tuple-element.37.refs_2_), channel_id=1, source_target_pairs={{1,0},{2,1},{3,2},{4,3},{5,4},{6,5},{7,6},{8,7},{9,8},{10,9},{11,1... | collective-permute-start | bytes 196616 | tf_op jit(solution)/shard_map/ppermute | solution.py:157
  13.4 7.9 %collective-permute-start.2 = (f32[64,256]{1,0:T(8,128)}, f32[64,256]{1,0:T(8,128)S(1)}, u32[]{:S(2)}, u32[]{:S(2)}) collective-permute-start(f32[64,256]{1,0:T(8,128)} %get-tuple-element.38.refs_3_), channel_id=1, source_target_pairs={{0,1},{1,2},{2,3},{3,4},{4,5},{5,6},{6,7},{7,8},{8,9},{9,10},{10,1... | collective-permute-start | bytes 196616 | tf_op jit(solution)/shard_map/ppermute | solution.py:156
  25.5 12.4 %collective-permute-start.5 = (f32[64,256]{1,0:T(8,128)}, f32[64,256]{1,0:T(8,128)S(1)}, u32[]{:S(2)}, u32[]{:S(2)}) collective-permute-start(f32[64,256]{1,0:T(8,128)} %get-tuple-element.39.refs_0_), channel_id=1, source_target_pairs={{64,0},{128,64},{192,128},{256,192},{320,256},{384,320},{448,384},... | collective-permute-start | bytes 196616 | tf_op jit(solution)/shard_map/ppermute | solution.py:157
  26.8 11.2 %collective-permute-start.4 = (f32[64,256]{1,0:T(8,128)}, f32[64,256]{1,0:T(8,128)S(1)}, u32[]{:S(2)}, u32[]{:S(2)}) collective-permute-start(f32[64,256]{1,0:T(8,128)} %get-tuple-element.40.refs_1_), channel_id=1, source_target_pairs={{0,64},{64,128},{128,192},{192,256},{256,320},{320,384},{384,448},... | collective-permute-start | bytes 196616 | tf_op jit(solution)/shard_map/ppermute | solution.py:156
  31.7 6.5 %collective-permute-start.7 = (f32[64,256]{1,0:T(8,128)}, f32[64,256]{1,0:T(8,128)S(1)}, u32[]{:S(2)}, u32[]{:S(2)}) collective-permute-start(f32[64,256]{1,0:T(8,128)} %get-tuple-element.41.refs_2_), channel_id=1, source_target_pairs={{1,0},{2,1},{3,2},{4,3},{5,4},{6,5},{7,6},{8,7},{9,8},{10,9},{11,1... | collective-permute-start | bytes 196616 | tf_op jit(solution)/shard_map/ppermute | solution.py:157
  36.0 7.9 %collective-permute-start.6 = (f32[64,256]{1,0:T(8,128)}, f32[64,256]{1,0:T(8,128)S(1)}, u32[]{:S(2)}, u32[]{:S(2)}) collective-permute-start(f32[64,256]{1,0:T(8,128)} %get-tuple-element.42.refs_3_), channel_id=1, source_target_pairs={{0,1},{1,2},{2,3},{3,4},{4,5},{5,6},{6,7},{7,8},{8,9},{9,10},{10,1... | collective-permute-start | bytes 196616 | tf_op jit(solution)/shard_map/ppermute | solution.py:156
  37.9 6.0 %copy-start.5 = (f32[64,256]{1,0:T(8,128)}, f32[64,256]{1,0:T(8,128)S(1)}, u32[]{:S(2)}) copy-start(f32[64,256]{1,0:T(8,128)S(1)} %collective-permute-done.5.refs_5_) | copy-start | bytes 196612
  37.9 6.0 %copy-start.9 = (f32[64,256]{1,0:T(8,128)}, f32[64,256]{1,0:T(8,128)S(1)}, u32[]{:S(2)}) copy-start(f32[64,256]{1,0:T(8,128)S(1)} %collective-permute-done.4.refs_4_) | copy-start | bytes 196612
  38.2 5.7 %copy-start.13 = (f32[64,256]{1,0:T(8,128)}, f32[64,256]{1,0:T(8,128)S(1)}, u32[]{:S(2)}) copy-start(f32[64,256]{1,0:T(8,128)S(1)} %collective-permute-done.7.refs_7_) | copy-start | bytes 196612
  48.3 10.5 %collective-permute-start.9 = (f32[64,256]{1,0:T(8,128)}, f32[64,256]{1,0:T(8,128)S(1)}, u32[]{:S(2)}, u32[]{:S(2)}) collective-permute-start(f32[64,256]{1,0:T(8,128)} %get-tuple-element.46.refs_0_), channel_id=1, source_target_pairs={{64,0},{128,64},{192,128},{256,192},{320,256},{384,320},{448,384},... | collective-permute-start | bytes 196616 | tf_op jit(solution)/shard_map/ppermute | solution.py:157
  49.6 9.3 %collective-permute-start.8 = (f32[64,256]{1,0:T(8,128)}, f32[64,256]{1,0:T(8,128)S(1)}, u32[]{:S(2)}, u32[]{:S(2)}) collective-permute-start(f32[64,256]{1,0:T(8,128)} %get-tuple-element.47.refs_1_), channel_id=1, source_target_pairs={{0,64},{64,128},{128,192},{192,256},{256,320},{320,384},{384,448},... | collective-permute-start | bytes 196616 | tf_op jit(solution)/shard_map/ppermute | solution.py:156
  54.5 4.4 %collective-permute-start.11 = (f32[64,256]{1,0:T(8,128)}, f32[64,256]{1,0:T(8,128)S(1)}, u32[]{:S(2)}, u32[]{:S(2)}) collective-permute-start(f32[64,256]{1,0:T(8,128)} %get-tuple-element.48.refs_2_), channel_id=1, source_target_pairs={{1,0},{2,1},{3,2},{4,3},{5,4},{6,5},{7,6},{8,7},{9,8},{10,9},{11,1... | collective-permute-start | bytes 196616 | tf_op jit(solution)/shard_map/ppermute | solution.py:157
  56.4 7.9 %collective-permute-start.10 = (f32[64,256]{1,0:T(8,128)}, f32[64,256]{1,0:T(8,128)S(1)}, u32[]{:S(2)}, u32[]{:S(2)}) collective-permute-start(f32[64,256]{1,0:T(8,128)} %get-tuple-element.49.refs_3_), channel_id=1, source_target_pairs={{0,1},{1,2},{2,3},{3,4},{4,5},{5,6},{6,7},{7,8},{8,9},{9,10},{10,1... | collective-permute-start | bytes 196616 | tf_op jit(solution)/shard_map/ppermute | solution.py:156
  58.8 5.5 %copy-start = (f32[64,256]{1,0:T(8,128)}, f32[64,256]{1,0:T(8,128)S(1)}, u32[]{:S(2)}) copy-start(f32[64,256]{1,0:T(8,128)S(1)} %collective-permute-done.9.refs_5_) | copy-start | bytes 196612
  58.9 5.5 %copy-start.2 = (f32[64,256]{1,0:T(8,128)}, f32[64,256]{1,0:T(8,128)S(1)}, u32[]{:S(2)}) copy-start(f32[64,256]{1,0:T(8,128)S(1)} %collective-permute-done.8.refs_4_) | copy-start | bytes 196612
  58.9 5.4 %copy-start.6 = (f32[64,256]{1,0:T(8,128)}, f32[64,256]{1,0:T(8,128)S(1)}, u32[]{:S(2)}) copy-start(f32[64,256]{1,0:T(8,128)S(1)} %collective-permute-done.11.refs_7_) | copy-start | bytes 196612
  84.0 29.7 %all-to-all-start.1 = ((f32[12,1,64]{2,1,0:T(1,128)}), f32[12,1,64]{2,1,0:T(1,128)S(1)}, u32[]{:S(2)}, u32[]{:S(2)}) async-start(f32[12,1,64]{2,1,0:T(1,128)} %broadcast_in_dim.20), calls=%async_computation.1 | async-start | bytes 12288 | tf_op jit(solution)/shard_map/all_to_all | solution.py:164
  103.6 10.8 %collective-permute-start.13 = (f32[64,256]{1,0:T(8,128)}, f32[64,256]{1,0:T(8,128)S(1)}, u32[]{:S(2)}, u32[]{:S(2)}) collective-permute-start(f32[64,256]{1,0:T(8,128)} %get-tuple-element.56.refs_0_), channel_id=1, source_target_pairs={{64,0},{128,64},{192,128},{256,192},{320,256},{384,320},{448,384},... | collective-permute-start | bytes 196616 | tf_op jit(solution)/shard_map/ppermute | solution.py:157
  104.9 9.5 %collective-permute-start.12 = (f32[64,256]{1,0:T(8,128)}, f32[64,256]{1,0:T(8,128)S(1)}, u32[]{:S(2)}, u32[]{:S(2)}) collective-permute-start(f32[64,256]{1,0:T(8,128)} %get-tuple-element.57.refs_1_), channel_id=1, source_target_pairs={{0,64},{64,128},{128,192},{192,256},{256,320},{320,384},{384,448},... | collective-permute-start | bytes 196616 | tf_op jit(solution)/shard_map/ppermute | solution.py:156
  109.4 4.9 %collective-permute-start.15 = (f32[64,256]{1,0:T(8,128)}, f32[64,256]{1,0:T(8,128)S(1)}, u32[]{:S(2)}, u32[]{:S(2)}) collective-permute-start(f32[64,256]{1,0:T(8,128)} %get-tuple-element.58.refs_2_), channel_id=1, source_target_pairs={{1,0},{2,1},{3,2},{4,3},{5,4},{6,5},{7,6},{8,7},{9,8},{10,9},{11,1... | collective-permute-start | bytes 196616 | tf_op jit(solution)/shard_map/ppermute | solution.py:157
  111.4 7.9 %collective-permute-start.14 = (f32[64,256]{1,0:T(8,128)}, f32[64,256]{1,0:T(8,128)S(1)}, u32[]{:S(2)}, u32[]{:S(2)}) collective-permute-start(f32[64,256]{1,0:T(8,128)} %get-tuple-element.59.refs_3_), channel_id=1, source_target_pairs={{0,1},{1,2},{2,3},{3,4},{4,5},{5,6},{6,7},{7,8},{8,9},{9,10},{10,1... | collective-permute-start | bytes 196616 | tf_op jit(solution)/shard_map/ppermute | solution.py:156
  114.4 4.9 %copy-start.3 = (f32[64,256]{1,0:T(8,128)}, f32[64,256]{1,0:T(8,128)S(1)}, u32[]{:S(2)}) copy-start(f32[64,256]{1,0:T(8,128)S(1)} %collective-permute-done.13.refs_5_) | copy-start | bytes 196612
  (9 other events, 16.2 us)

commit v2 on v1

--- a/solution.py
+++ b/solution.py
@@ -7,6 +7,7 @@
 from jax.experimental import pallas as pl
 from jax.experimental.pallas import tpu as pltpu
 from jax.sharding import PartitionSpec as P
+
 
 IFACE = 1024
 FACE = 256
@@ -17,8 +18,11 @@
 CONTACT = 128
 F32 = jnp.float32
 BF16 = jnp.bfloat16
+LIMIT = 20 * 1024 * 1024
 VM = pl.BlockSpec(memory_space=pltpu.VMEM)
 SM = pl.BlockSpec(memory_space=pltpu.SMEM)
+HB = pl.BlockSpec(memory_space=pltpu.HBM)
+CHUNKS = 4
 NN = (((1,), (0,)), ((), ()))
 NT = (((1,), (1,)), ((), ()))
 
@@ -54,28 +58,46 @@
     return (row == table_row).astype(F32).astype(BF16)
 
 
-def live_slots(lengths, face):
+def fetch(pairs, sems):
+    copies = []
+    for index, (source, target) in enumerate(pairs):
+        copies.append(pltpu.make_async_copy(source, target, sems.at[index]))
+        copies[-1].start()
+    return copies
+
+
+def loads_kernel(lengths_hbm, table_hbm, loads_hbm, perm, live, *refs):
+    sends, (lengths, table, loads, sems) = refs[0:4], refs[4:]
+    pairs = [(lengths_hbm, lengths), (table_hbm, table), (loads_hbm, loads)]
+    lengths_copy, table_copy, loads_copy = fetch(pairs, sems)
+    lengths_copy.wait()
     slot = lax.broadcasted_iota(jnp.int32, (1, FACE), 1)
-    return (slot < lengths[0, face]).astype(F32)
-
-
-def loads_kernel(lengths, table, loads, perm, *sends):
-    for face in range(4):
-        hot = one_hot(table[face : face + 1, :])
-        perm[face] = hot
-        part = loads[:, face * FACE : (face + 1) * FACE]
-        sends[face][...] = stacked_dot(part, hot, NN, 3) * live_slots(lengths, face)
-
-
-def panel_kernel(enrich, panel, perm, compliance, contact, kept, diag, counts):
-    live_rows = enrich[0, 0] * BLOCK_ROWS
-    keep = lax.broadcasted_iota(jnp.int32, (ROWS, FACE), 0) < live_rows
+    for face in range(4):
+        live[:, face * FACE : (face + 1) * FACE] = (slot < lengths[0, face]).astype(F32)
+    table_copy.wait()
+    hots = [one_hot(table[face : face + 1, :]) for face in range(4)]
+    for face in range(4):
+        perm[face] = hots[face]
+    loads_copy.wait()
+    for face in range(4):
+        cols = slice(face * FACE, (face + 1) * FACE)
+        sends[face][...] = stacked_dot(loads[:, cols], hots[face], NN, 3) * live[:, cols]
+
+
+def panel_kernel(enrich, panel_hbm, diag_hbm, contact_hbm, perm, kept, diag, counts, *refs):
+    panel, local_diag, contact, sems = refs
+    height = ROWS // CHUNKS
+    pairs = [(diag_hbm, local_diag), (contact_hbm, contact)]
+    for chunk in range(CHUNKS):
+        rows = pl.ds(chunk * height, height)
+        pairs.append((panel_hbm.at[rows], panel.at[rows]))
+    copies = fetch(pairs, sems)
+    for copy in copies[0:2]:
+        copy.wait()
     across = jnp.broadcast_to(contact[...], (CONTACT, CONTACT)).T
     for face in range(4):
         cols = slice(face * FACE, (face + 1) * FACE)
-        moved = lax.dot_general(panel[:, cols], perm[face], NN, preferred_element_type=F32)
-        kept[:, cols] = jnp.where(keep, moved, 0.0).astype(BF16)
-        part = jnp.broadcast_to(compliance[:, cols], (8, FACE))
+        part = jnp.broadcast_to(local_diag[:, cols], (8, FACE))
         diag[:, cols] = stacked_dot(part, perm[face], NN, 3)[0:1]
         tallies = []
         for half in range(FACE // CONTACT):
@@ -84,9 +106,26 @@
             tallies.append(jnp.sum((across == index).astype(F32), axis=0, keepdims=True))
         tally = jnp.broadcast_to(jnp.concatenate(tallies, axis=1), (8, FACE)).astype(BF16)
         counts[:, cols] = lax.dot_general(tally, perm[face], NN, preferred_element_type=F32)[0:1]
-
-
-def step_kernel(first, last, keep_dir, add_res, lengths, kept, diag, *refs):
+    for chunk in range(CHUNKS):
+        rows = slice(chunk * height, (chunk + 1) * height)
+        copies[2 + chunk].wait()
+        block = chunk * height // BLOCK_ROWS
+
+        @pl.when(block < enrich[0, 0])
+        def _():
+            for face in range(4):
+                cols = slice(face * FACE, (face + 1) * FACE)
+                moved = lax.dot_general(
+                    panel[rows, cols], perm[face], NN, preferred_element_type=F32
+                )
+                kept[rows, cols] = moved.astype(BF16)
+
+        @pl.when(block >= enrich[0, 0])
+        def _():
+            kept[rows, :] = jnp.zeros((height, IFACE), BF16)
+
+
+def step_kernel(first, last, keep_dir, add_res, live, kept, diag, *refs):
     own, got = refs[0:4], refs[4:8]
     refs = refs[8:]
     assembled = jnp.concatenate([o[...] + g[...] for o, g in zip(own, got)], axis=1)
@@ -110,7 +149,7 @@
     image = stacked_dot(projected, kept[...], NN, 2) + direction * diag[...]
     for face in range(4):
         cols = slice(face * FACE, (face + 1) * FACE)
-        sends[face][...] = image[:, cols] * live_slots(lengths, face)
+        sends[face][...] = image[:, cols] * live[:, cols]
     if last:
         negative = jnp.minimum(solution, 0.0)
         weights = jnp.broadcast_to(counts[...], (8, IFACE)).astype(BF16)
@@ -120,7 +159,7 @@
             piece = square.astype(BF16)
             square = square - piece.astype(F32)
             terms = terms + lax.dot_general(weights, piece, NT, preferred_element_type=F32)
-        refs[7][...] = jnp.broadcast_to(terms[0:1], refs[7].shape)
+        refs[7][...] = jnp.broadcast_to(terms[0:1][None], refs[7].shape)
 
 
 def solution_kernel(perm, field, out):
@@ -137,14 +176,19 @@
         out[:, cols] = stacked_dot(value, perm[face], NT, 3)
 
 
-def call(body, name, out_shapes, in_specs):
+def call(body, out_shapes, in_specs, scratch=()):
     return pl.pallas_call(
         body,
-        name=name,
         out_shape=[jax.ShapeDtypeStruct(shape, dtype) for shape, dtype in out_shapes],
         in_specs=in_specs,
+        scratch_shapes=scratch,
         out_specs=[VM] * len(out_shapes),
+        compiler_params=pltpu.CompilerParams(vmem_limit_bytes=LIMIT),
     )
+
+
+def in_hbm(array):
+    return pltpu.with_memory_space_constraint(array, pltpu.HBM)
 
 
 def exchange(sends):
@@ -158,50 +202,57 @@
     return got
 
 
-def total_over(row, axis):
-    count = lax.axis_size(axis)
-    spread = jnp.broadcast_to(row[None, :], (count, row.shape[0]))
-    return jnp.sum(lax.all_to_all(spread, axis, 0, 0), axis=0)
-
-
 def local(panels, enrich, compliance, loads, face_maps, face_lengths, contact):
-    lengths = face_lengths.reshape(1, 4)
     center, half_span, ratio = chebyshev_constants()
     face_field = ((LOADS, FACE), F32)
     field = ((LOADS, IFACE), F32)
-    perm, *sends = call(
-        loads_kernel, "loads", [((4, FACE, FACE), BF16)] + [face_field] * 4, [SM, VM, VM]
-    )(lengths, face_maps[0, 0], loads[0, 0])
+    flag = ((1, IFACE), F32)
+    perm, live, *sends = call(
+        loads_kernel,
+        [((4, FACE, FACE), BF16), flag] + [face_field] * 4,
+        [HB] * 3,
+        [
+            pltpu.SMEM((1, 4), jnp.int32),
+            pltpu.VMEM((4, FACE), jnp.int32),
+            pltpu.VMEM((LOADS, IFACE), F32),
+            pltpu.SemaphoreType.DMA((3,)),
+        ],
+    )(in_hbm(face_lengths[0]), in_hbm(face_maps[0, 0]), in_hbm(loads[0, 0]))
     got = exchange(sends)
     kept, diag, counts = call(
         panel_kernel,
-        "panel",
-        [((ROWS, IFACE), BF16), ((1, IFACE), F32), ((1, IFACE), F32)],
-        [SM, VM, VM, VM, VM],
-    )(enrich, panels[0, 0], perm, compliance[0], contact[0])
+        [((ROWS, IFACE), BF16), flag, flag],
+        [SM] + [HB] * 3 + [VM],
+        [
+            pltpu.VMEM((ROWS, IFACE), BF16),
+            pltpu.VMEM((1, IFACE), F32),
+            pltpu.VMEM((1, CONTACT), jnp.int32),
+            pltpu.SemaphoreType.DMA((CHUNKS + 2,)),
+        ],
+    )(enrich, in_hbm(panels[0, 0]), in_hbm(compliance[0]), in_hbm(contact[0]), perm)
     state = []
     rho = 1.0 / ratio
     keep_dir, add_res = 0.0, 1.0 / center
     for iteration in range(ITERS):
         last = iteration + 1 == ITERS
-        inputs = [lengths, kept, diag, *sends, *got, *state] + ([counts] if last else [])
+        inputs = [live, kept, diag, *sends, *got, *state] + ([counts] if last else [])
         outs = call(
             functools.partial(step_kernel, iteration == 0, last, keep_dir, add_res),
-            "step",
-            [field] * 3 + [face_field] * 4 + ([((8, LOADS), F32)] if last else []),
-            [SM] + [VM] * (len(inputs) - 1),
+            [field] * 3 + [face_field] * 4 + ([((lax.axis_size("bal"), 1, LOADS), F32)] if last else []),
+            [VM] * len(inputs),
         )(*inputs)
         state, sends = outs[0:3], outs[3:7]
         got = exchange(sends)
         rho_next = 1.0 / (2.0 * ratio - rho)
         keep_dir, add_res = rho_next * rho, 2.0 * rho_next / half_span
         rho = rho_next
-    terms = outs[7][0]
-    (solved,) = call(solution_kernel, "solved", [field], [VM, VM])(perm, state[2])
-    (residual,) = call(residual_kernel, "residual", [field], [VM] * 10)(
-        perm, state[0], *sends, *got
-    )
-    violation = jnp.sqrt(total_over(total_over(terms, "bal"), "space") + 1e-06)
+    heard = lax.all_to_all(outs[7], "bal", 0, 0)
+    part = jnp.sum(heard, axis=0, keepdims=True)
+    spread = jnp.broadcast_to(part, (lax.axis_size("space"), 1, LOADS))
+    heard = lax.all_to_all(spread, "space", 0, 0)
+    (solved,) = call(solution_kernel, [field], [VM, VM])(perm, state[2])
+    (residual,) = call(residual_kernel, [field], [VM] * 10)(perm, state[0], *sends, *got)
+    violation = jnp.sqrt(jnp.sum(heard[:, 0], axis=0) + 1e-06)
     return (solved[None, None], residual[None, None], violation)
 
 
@@ -216,4 +267,5 @@
         P("space", "bal", None),
     )
     out_specs = (P("space", "bal", None, None), P("space", "bal", None, None), P())
+
     return jax.shard_map(local, mesh=mesh, in_specs=in_specs, out_specs=out_specs, check_vma=False)

time: 123 us -> 107 us (0.87)
  Pallas kernels: 21.8 us -> 9.45 us
  local copies, waits for them, and re-layouts: 3.76 us -> 0.6 us
  waiting for transfers between devices: 17.5 us -> 19 us
    pallas_call x3, Pallas kernels: 11.3 us -> 4.28 us  [local(): call(functools.partial(step_kernel, iteration == 0, last, keep_dir, add_r...]
    pallas_call x4, Pallas kernels: 10.5 us -> 5.17 us  [the longest x1 1.84 us: local(): call(panel_kernel, [((ROWS, IFACE), BF16), flag, flag], [SM] + [HB] * 3 +...]
    unnamed x32 -> x0, local copies, waits for them, and re-layouts: 2.47 us -> none
    ppermute x8, waiting for transfers between devices: 17.3 us -> 19 us  [exchange(): got[low] = lax.ppermute(sends[low + 1], axis, forward)]
    ppermute x8, starting transfers between devices: 17.8 us -> 16.3 us  [exchange(): got[low + 1] = lax.ppermute(sends[low], axis, backward)]
  transfers between devices with their start and end apart: 17 -> 17, of which waited for: 5 -> 4; matrix products, arithmetic and copies ran while one was open for 0% -> 1% of each run, Pallas kernels for 5% -> 3%
where the time goes in v2:
time: 107 us
  starting transfers between devices  61.9 us (58%)
  waiting for transfers between devices  19 us (18%)
  blocking collectives  13.5 us (13%)
  Pallas kernels  9.45 us (9%)
  between operations  1.53 us (1%)
    ppermute x8, starting transfers between devices, exchange(): got[low] = lax.ppermute(sends[low + 1], axis, forward)  27.9 us
    ppermute x8, waiting for transfers between devices, exchange(): got[low] = lax.ppermute(sends[low + 1], axis, forward)  19 us
    all_to_all x1, starting transfers between devices, local(): heard = lax.all_to_all(spread, 'space', 0, 0)  17.7 us
    ppermute x8, starting transfers between devices, exchange(): got[low + 1] = lax.ppermute(sends[low], axis, backward)  16.3 us
    all_to_all x1, blocking collectives, local(): heard = lax.all_to_all(outs[7], 'bal', 0, 0)  13.5 us
    pallas_call x3, Pallas kernels, local(): call(functools.partial(step_kernel, iteration == 0, last, keep_dir, add_r...  4.28 us
  transfers between devices with their start and end apart: 17, of which 4 were waited for; matrix products, arithmetic and copies ran while one was open for 1% of the time, Pallas kernels for 3%

profile of v2, /device:TPU:2, one launch (start us, length us, event | category | flops | bytes accessed | tf_op | source)
XLA Modules:
  0.0 106.6 jit_solution(6254614838508325608)
XLA Ops:
  1.9 1.3 %collective-permute-start.1 = (f32[64,256]{1,0:T(8,128)S(1)}, f32[64,256]{1,0:T(8,128)S(1)}, u32[]{:S(2)}, u32[]{:S(2)}) collective-permute-start(f32[64,256]{1,0:T(8,128)S(1)} %get-tuple-element.37.refs_0_), channel_id=1, source_target_pairs={{64,0},{128,64},{192,128},{256,192},{320,256},{384,320},{448,384},... | collective-permute-start | bytes 196616 | tf_op jit(solution)/shard_map/ppermute | solution.py:201
  3.2 4.9 %collective-permute-start = (f32[64,256]{1,0:T(8,128)S(1)}, f32[64,256]{1,0:T(8,128)S(1)}, u32[]{:S(2)}, u32[]{:S(2)}) collective-permute-start(f32[64,256]{1,0:T(8,128)S(1)} %get-tuple-element.38.refs_1_), channel_id=1, source_target_pairs={{0,64},{64,128},{128,192},{192,256},{256,320},{320,384},{384,448},... | collective-permute-start | bytes 196616 | tf_op jit(solution)/shard_map/ppermute | solution.py:200
  8.1 4.5 %collective-permute-start.3 = (f32[64,256]{1,0:T(8,128)S(1)}, f32[64,256]{1,0:T(8,128)S(1)}, u32[]{:S(2)}, u32[]{:S(2)}) collective-permute-start(f32[64,256]{1,0:T(8,128)S(1)} %get-tuple-element.39.refs_2_), channel_id=1, source_target_pairs={{1,0},{2,1},{3,2},{4,3},{5,4},{6,5},{7,6},{8,7},{9,8},{10,9},{11,1... | collective-permute-start | bytes 196616 | tf_op jit(solution)/shard_map/ppermute | solution.py:201
  12.6 1.9 %collective-permute-start.2 = (f32[64,256]{1,0:T(8,128)S(1)}, f32[64,256]{1,0:T(8,128)S(1)}, u32[]{:S(2)}, u32[]{:S(2)}) collective-permute-start(f32[64,256]{1,0:T(8,128)S(1)} %get-tuple-element.40.refs_3_), channel_id=1, source_target_pairs={{0,1},{1,2},{2,3},{3,4},{4,5},{5,6},{6,7},{7,8},{8,9},{9,10},{10,1... | collective-permute-start | bytes 196616 | tf_op jit(solution)/shard_map/ppermute | solution.py:200
  15.2 1.8 %shard_map.95 = (bf16[1024,1024]{1,0:T(8,128)(2,1)S(1)}, f32[1,1024]{1,0:T(1,128)S(1)}, f32[1,1024]{1,0:T(1,128)S(1)}) custom-call(s32[1,1]{1,0:T(1,128)S(6)} %copy.10.enrich, bf16[1024,1024]{1,0:T(8,128)(2,1)} %bitcast.8, f32[1,1024]{1,0:T(1,128)} %bitcast.13, s32[1,128]{1,0:T(1,128)} %bitcast.15, bf16[4,256,256]{2,1,0:T(8,128)(2,1)S(1)} %get-tuple-element.33.perm), custom_call_target="tpu_custom_call" | custom-call | tf_op jit(solution)/shard_map/pallas_call | solution.py:222
  17.1 3.2 %collective-permute-done.2.refs_6_ = f32[64,256]{1,0:T(8,128)S(1)} collective-permute-done((f32[64,256]{1,0:T(8,128)S(1)}, f32[64,256]{1,0:T(8,128)S(1)}, u32[]{:S(2)}, u32[]{:S(2)}) %collective-permute-start.2) | collective-permute-done | bytes 65568 | tf_op jit(solution)/shard_map/ppermute | solution.py:200
  21.5 1.3 %collective-permute-start.5 = (f32[64,256]{1,0:T(8,128)S(1)}, f32[64,256]{1,0:T(8,128)S(1)}, u32[]{:S(2)}, u32[]{:S(2)}) collective-permute-start(f32[64,256]{1,0:T(8,128)S(1)} %get-tuple-element.41.refs_0_), channel_id=1, source_target_pairs={{64,0},{128,64},{192,128},{256,192},{320,256},{384,320},{448,384},... | collective-permute-start | bytes 196616 | tf_op jit(solution)/shard_map/ppermute | solution.py:201
  22.8 4.9 %collective-permute-start.4 = (f32[64,256]{1,0:T(8,128)S(1)}, f32[64,256]{1,0:T(8,128)S(1)}, u32[]{:S(2)}, u32[]{:S(2)}) collective-permute-start(f32[64,256]{1,0:T(8,128)S(1)} %get-tuple-element.42.refs_1_), channel_id=1, source_target_pairs={{0,64},{64,128},{128,192},{192,256},{256,320},{320,384},{384,448},... | collective-permute-start | bytes 196616 | tf_op jit(solution)/shard_map/ppermute | solution.py:200
  27.7 2.8 %collective-permute-start.7 = (f32[64,256]{1,0:T(8,128)S(1)}, f32[64,256]{1,0:T(8,128)S(1)}, u32[]{:S(2)}, u32[]{:S(2)}) collective-permute-start(f32[64,256]{1,0:T(8,128)S(1)} %get-tuple-element.43.refs_2_), channel_id=1, source_target_pairs={{1,0},{2,1},{3,2},{4,3},{5,4},{6,5},{7,6},{8,7},{9,8},{10,9},{11,1... | collective-permute-start | bytes 196616 | tf_op jit(solution)/shard_map/ppermute | solution.py:201
  30.5 1.9 %collective-permute-start.6 = (f32[64,256]{1,0:T(8,128)S(1)}, f32[64,256]{1,0:T(8,128)S(1)}, u32[]{:S(2)}, u32[]{:S(2)}) collective-permute-start(f32[64,256]{1,0:T(8,128)S(1)} %get-tuple-element.44.refs_3_), channel_id=1, source_target_pairs={{0,1},{1,2},{2,3},{3,4},{4,5},{5,6},{6,7},{7,8},{8,9},{9,10},{10,1... | collective-permute-start | bytes 196616 | tf_op jit(solution)/shard_map/ppermute | solution.py:200
  32.5 5.7 %collective-permute-done.6.refs_6_ = f32[64,256]{1,0:T(8,128)S(1)} collective-permute-done((f32[64,256]{1,0:T(8,128)S(1)}, f32[64,256]{1,0:T(8,128)S(1)}, u32[]{:S(2)}, u32[]{:S(2)}) %collective-permute-start.6) | collective-permute-done | bytes 65568 | tf_op jit(solution)/shard_map/ppermute | solution.py:200
  39.4 1.3 %collective-permute-start.9 = (f32[64,256]{1,0:T(8,128)S(1)}, f32[64,256]{1,0:T(8,128)S(1)}, u32[]{:S(2)}, u32[]{:S(2)}) collective-permute-start(f32[64,256]{1,0:T(8,128)S(1)} %get-tuple-element.48.refs_0_), channel_id=1, source_target_pairs={{64,0},{128,64},{192,128},{256,192},{320,256},{384,320},{448,384},... | collective-permute-start | bytes 196616 | tf_op jit(solution)/shard_map/ppermute | solution.py:201
  40.7 4.9 %collective-permute-start.8 = (f32[64,256]{1,0:T(8,128)S(1)}, f32[64,256]{1,0:T(8,128)S(1)}, u32[]{:S(2)}, u32[]{:S(2)}) collective-permute-start(f32[64,256]{1,0:T(8,128)S(1)} %get-tuple-element.49.refs_1_), channel_id=1, source_target_pairs={{0,64},{64,128},{128,192},{192,256},{256,320},{320,384},{384,448},... | collective-permute-start | bytes 196616 | tf_op jit(solution)/shard_map/ppermute | solution.py:200
  45.6 1.9 %collective-permute-start.11 = (f32[64,256]{1,0:T(8,128)S(1)}, f32[64,256]{1,0:T(8,128)S(1)}, u32[]{:S(2)}, u32[]{:S(2)}) collective-permute-start(f32[64,256]{1,0:T(8,128)S(1)} %get-tuple-element.50.refs_2_), channel_id=1, source_target_pairs={{1,0},{2,1},{3,2},{4,3},{5,4},{6,5},{7,6},{8,7},{9,8},{10,9},{11,1... | collective-permute-start | bytes 196616 | tf_op jit(solution)/shard_map/ppermute | solution.py:201
  47.5 2.4 %collective-permute-start.10 = (f32[64,256]{1,0:T(8,128)S(1)}, f32[64,256]{1,0:T(8,128)S(1)}, u32[]{:S(2)}, u32[]{:S(2)}) collective-permute-start(f32[64,256]{1,0:T(8,128)S(1)} %get-tuple-element.51.refs_3_), channel_id=1, source_target_pairs={{0,1},{1,2},{2,3},{3,4},{4,5},{5,6},{6,7},{7,8},{8,9},{9,10},{10,1... | collective-permute-start | bytes 196616 | tf_op jit(solution)/shard_map/ppermute | solution.py:200
  50.0 5.2 %collective-permute-done.10.refs_6_ = f32[64,256]{1,0:T(8,128)S(1)} collective-permute-done((f32[64,256]{1,0:T(8,128)S(1)}, f32[64,256]{1,0:T(8,128)S(1)}, u32[]{:S(2)}, u32[]{:S(2)}) %collective-permute-start.10) | collective-permute-done | bytes 65568 | tf_op jit(solution)/shard_map/ppermute | solution.py:200
  55.2 1.9 %shard_map.98 = (f32[64,1024]{1,0:T(8,128)S(1)}, f32[64,1024]{1,0:T(8,128)}, f32[64,1024]{1,0:T(8,128)S(1)}, f32[64,256]{1,0:T(8,128)S(1)}, f32[64,256]{1,0:T(8,...) custom-call(f32[1,1024]{1,0:T(1,128)S(1)} %get-tuple-element.34.live, ...), custom_call_target="tpu_custom_call" | custom-call | tf_op jit(solution)/shard_map/pallas_call | solution.py:239
  57.2 13.5 %all_to_all.10 = f32[64,1,64]{2,1,0:T(1,128)S(1)} all-to-all(f32[64,1,64]{2,1,0:T(1,128)S(1)} %get-tuple-element.62), channel_id=1, replica_groups=mesh['space'=12,'bal'=64] {'bal'}, dimensions={0} | all-to-all | bytes 32768 | tf_op jit(solution)/shard_map/all_to_all | solution.py:249
  71.3 17.7 %all-to-all-start.1 = ((f32[12,1,64]{2,1,0:T(1,128)}), f32[12,1,64]{2,1,0:T(1,128)S(1)}, u32[]{:S(2)}, u32[]{:S(2)}) async-start(f32[12,1,64]{2,1,0:T(1,128)} %broadcast_in_dim.14), calls=%async_computation.1 | async-start | bytes 12288 | tf_op jit(solution)/shard_map/all_to_all | solution.py:252
  90.1 1.3 %collective-permute-start.13 = (f32[64,256]{1,0:T(8,128)S(1)}, f32[64,256]{1,0:T(8,128)S(1)}, u32[]{:S(2)}, u32[]{:S(2)}) collective-permute-start(f32[64,256]{1,0:T(8,128)S(1)} %get-tuple-element.58.refs_0_), channel_id=1, source_target_pairs={{64,0},{128,64},{192,128},{256,192},{320,256},{384,320},{448,384},... | collective-permute-start | bytes 196616 | tf_op jit(solution)/shard_map/ppermute | solution.py:201
  91.4 4.5 %collective-permute-start.12 = (f32[64,256]{1,0:T(8,128)S(1)}, f32[64,256]{1,0:T(8,128)S(1)}, u32[]{:S(2)}, u32[]{:S(2)}) collective-permute-start(f32[64,256]{1,0:T(8,128)S(1)} %get-tuple-element.59.refs_1_), channel_id=1, source_target_pairs={{0,64},{64,128},{128,192},{192,256},{256,320},{320,384},{384,448},... | collective-permute-start | bytes 196616 | tf_op jit(solution)/shard_map/ppermute | solution.py:200
  95.9 1.9 %collective-permute-start.15 = (f32[64,256]{1,0:T(8,128)S(1)}, f32[64,256]{1,0:T(8,128)S(1)}, u32[]{:S(2)}, u32[]{:S(2)}) collective-permute-start(f32[64,256]{1,0:T(8,128)S(1)} %get-tuple-element.60.refs_2_), channel_id=1, source_target_pairs={{1,0},{2,1},{3,2},{4,3},{5,4},{6,5},{7,6},{8,7},{9,8},{10,9},{11,1... | collective-permute-start | bytes 196616 | tf_op jit(solution)/shard_map/ppermute | solution.py:201
  97.9 2.4 %collective-permute-start.14 = (f32[64,256]{1,0:T(8,128)S(1)}, f32[64,256]{1,0:T(8,128)S(1)}, u32[]{:S(2)}, u32[]{:S(2)}) collective-permute-start(f32[64,256]{1,0:T(8,128)S(1)} %get-tuple-element.61.refs_3_), channel_id=1, source_target_pairs={{0,1},{1,2},{2,3},{3,4},{4,5},{5,6},{6,7},{7,8},{8,9},{9,10},{10,1... | collective-permute-start | bytes 196616 | tf_op jit(solution)/shard_map/ppermute | solution.py:200
  100.9 4.7 %collective-permute-done.14.refs_6_ = f32[64,256]{1,0:T(8,128)S(1)} collective-permute-done((f32[64,256]{1,0:T(8,128)S(1)}, f32[64,256]{1,0:T(8,128)S(1)}, u32[]{:S(2)}, u32[]{:S(2)}) %collective-permute-start.14) | collective-permute-done | bytes 65568 | tf_op jit(solution)/shard_map/ppermute | solution.py:200
  (22 shorter events, 7.0 us)
Async XLA Ops:
  1.9 15.2 %collective-permute-start.1 = (f32[64,256]{1,0:T(8,128)S(1)}, f32[64,256]{1,0:T(8,128)S(1)}, u32[]{:S(2)}, u32[]{:S(2)}) collective-permute-start(f32[64,256]{1,0:T(8,128)S(1)} %get-tuple-element.37.refs_0_), channel_id=1, source_target_pairs={{64,0},{128,64},{192,128},{256,192},{320,256},{384,320},{448,384},... | collective-permute-start | bytes 196616 | tf_op jit(solution)/shard_map/ppermute | solution.py:201
  3.2 13.9 %collective-permute-start = (f32[64,256]{1,0:T(8,128)S(1)}, f32[64,256]{1,0:T(8,128)S(1)}, u32[]{:S(2)}, u32[]{:S(2)}) collective-permute-start(f32[64,256]{1,0:T(8,128)S(1)} %get-tuple-element.38.refs_1_), channel_id=1, source_target_pairs={{0,64},{64,128},{128,192},{192,256},{256,320},{320,384},{384,448},... | collective-permute-start | bytes 196616 | tf_op jit(solution)/shard_map/ppermute | solution.py:200
  8.1 9.0 %collective-permute-start.3 = (f32[64,256]{1,0:T(8,128)S(1)}, f32[64,256]{1,0:T(8,128)S(1)}, u32[]{:S(2)}, u32[]{:S(2)}) collective-permute-start(f32[64,256]{1,0:T(8,128)S(1)} %get-tuple-element.39.refs_2_), channel_id=1, source_target_pairs={{1,0},{2,1},{3,2},{4,3},{5,4},{6,5},{7,6},{8,7},{9,8},{10,9},{11,1... | collective-permute-start | bytes 196616 | tf_op jit(solution)/shard_map/ppermute | solution.py:201
  12.6 7.7 %collective-permute-start.2 = (f32[64,256]{1,0:T(8,128)S(1)}, f32[64,256]{1,0:T(8,128)S(1)}, u32[]{:S(2)}, u32[]{:S(2)}) collective-permute-start(f32[64,256]{1,0:T(8,128)S(1)} %get-tuple-element.40.refs_3_), channel_id=1, source_target_pairs={{0,1},{1,2},{2,3},{3,4},{4,5},{5,6},{6,7},{7,8},{8,9},{9,10},{10,1... | collective-permute-start | bytes 196616 | tf_op jit(solution)/shard_map/ppermute | solution.py:200
  21.5 10.9 %collective-permute-start.5 = (f32[64,256]{1,0:T(8,128)S(1)}, f32[64,256]{1,0:T(8,128)S(1)}, u32[]{:S(2)}, u32[]{:S(2)}) collective-permute-start(f32[64,256]{1,0:T(8,128)S(1)} %get-tuple-element.41.refs_0_), channel_id=1, source_target_pairs={{64,0},{128,64},{192,128},{256,192},{320,256},{384,320},{448,384},... | collective-permute-start | bytes 196616 | tf_op jit(solution)/shard_map/ppermute | solution.py:201
  22.8 9.7 %collective-permute-start.4 = (f32[64,256]{1,0:T(8,128)S(1)}, f32[64,256]{1,0:T(8,128)S(1)}, u32[]{:S(2)}, u32[]{:S(2)}) collective-permute-start(f32[64,256]{1,0:T(8,128)S(1)} %get-tuple-element.42.refs_1_), channel_id=1, source_target_pairs={{0,64},{64,128},{128,192},{192,256},{256,320},{320,384},{384,448},... | collective-permute-start | bytes 196616 | tf_op jit(solution)/shard_map/ppermute | solution.py:200
  27.7 4.7 %collective-permute-start.7 = (f32[64,256]{1,0:T(8,128)S(1)}, f32[64,256]{1,0:T(8,128)S(1)}, u32[]{:S(2)}, u32[]{:S(2)}) collective-permute-start(f32[64,256]{1,0:T(8,128)S(1)} %get-tuple-element.43.refs_2_), channel_id=1, source_target_pairs={{1,0},{2,1},{3,2},{4,3},{5,4},{6,5},{7,6},{8,7},{9,8},{10,9},{11,1... | collective-permute-start | bytes 196616 | tf_op jit(solution)/shard_map/ppermute | solution.py:201
  30.5 7.7 %collective-permute-start.6 = (f32[64,256]{1,0:T(8,128)S(1)}, f32[64,256]{1,0:T(8,128)S(1)}, u32[]{:S(2)}, u32[]{:S(2)}) collective-permute-start(f32[64,256]{1,0:T(8,128)S(1)} %get-tuple-element.44.refs_3_), channel_id=1, source_target_pairs={{0,1},{1,2},{2,3},{3,4},{4,5},{5,6},{6,7},{7,8},{8,9},{9,10},{10,1... | collective-permute-start | bytes 196616 | tf_op jit(solution)/shard_map/ppermute | solution.py:200
  39.4 10.6 %collective-permute-start.9 = (f32[64,256]{1,0:T(8,128)S(1)}, f32[64,256]{1,0:T(8,128)S(1)}, u32[]{:S(2)}, u32[]{:S(2)}) collective-permute-start(f32[64,256]{1,0:T(8,128)S(1)} %get-tuple-element.48.refs_0_), channel_id=1, source_target_pairs={{64,0},{128,64},{192,128},{256,192},{320,256},{384,320},{448,384},... | collective-permute-start | bytes 196616 | tf_op jit(solution)/shard_map/ppermute | solution.py:201
  40.7 9.3 %collective-permute-start.8 = (f32[64,256]{1,0:T(8,128)S(1)}, f32[64,256]{1,0:T(8,128)S(1)}, u32[]{:S(2)}, u32[]{:S(2)}) collective-permute-start(f32[64,256]{1,0:T(8,128)S(1)} %get-tuple-element.49.refs_1_), channel_id=1, source_target_pairs={{0,64},{64,128},{128,192},{192,256},{256,320},{320,384},{384,448},... | collective-permute-start | bytes 196616 | tf_op jit(solution)/shard_map/ppermute | solution.py:200
  45.6 4.4 %collective-permute-start.11 = (f32[64,256]{1,0:T(8,128)S(1)}, f32[64,256]{1,0:T(8,128)S(1)}, u32[]{:S(2)}, u32[]{:S(2)}) collective-permute-start(f32[64,256]{1,0:T(8,128)S(1)} %get-tuple-element.50.refs_2_), channel_id=1, source_target_pairs={{1,0},{2,1},{3,2},{4,3},{5,4},{6,5},{7,6},{8,7},{9,8},{10,9},{11,1... | collective-permute-start | bytes 196616 | tf_op jit(solution)/shard_map/ppermute | solution.py:201
  47.5 7.7 %collective-permute-start.10 = (f32[64,256]{1,0:T(8,128)S(1)}, f32[64,256]{1,0:T(8,128)S(1)}, u32[]{:S(2)}, u32[]{:S(2)}) collective-permute-start(f32[64,256]{1,0:T(8,128)S(1)} %get-tuple-element.51.refs_3_), channel_id=1, source_target_pairs={{0,1},{1,2},{2,3},{3,4},{4,5},{5,6},{6,7},{7,8},{8,9},{9,10},{10,1... | collective-permute-start | bytes 196616 | tf_op jit(solution)/shard_map/ppermute | solution.py:200
  71.3 29.0 %all-to-all-start.1 = ((f32[12,1,64]{2,1,0:T(1,128)}), f32[12,1,64]{2,1,0:T(1,128)S(1)}, u32[]{:S(2)}, u32[]{:S(2)}) async-start(f32[12,1,64]{2,1,0:T(1,128)} %broadcast_in_dim.14), calls=%async_computation.1 | async-start | bytes 12288 | tf_op jit(solution)/shard_map/all_to_all | solution.py:252
  90.1 10.8 %collective-permute-start.13 = (f32[64,256]{1,0:T(8,128)S(1)}, f32[64,256]{1,0:T(8,128)S(1)}, u32[]{:S(2)}, u32[]{:S(2)}) collective-permute-start(f32[64,256]{1,0:T(8,128)S(1)} %get-tuple-element.58.refs_0_), channel_id=1, source_target_pairs={{64,0},{128,64},{192,128},{256,192},{320,256},{384,320},{448,384},... | collective-permute-start | bytes 196616 | tf_op jit(solution)/shard_map/ppermute | solution.py:201
  91.4 9.5 %collective-permute-start.12 = (f32[64,256]{1,0:T(8,128)S(1)}, f32[64,256]{1,0:T(8,128)S(1)}, u32[]{:S(2)}, u32[]{:S(2)}) collective-permute-start(f32[64,256]{1,0:T(8,128)S(1)} %get-tuple-element.59.refs_1_), channel_id=1, source_target_pairs={{0,64},{64,128},{128,192},{192,256},{256,320},{320,384},{384,448},... | collective-permute-start | bytes 196616 | tf_op jit(solution)/shard_map/ppermute | solution.py:200
  95.9 4.9 %collective-permute-start.15 = (f32[64,256]{1,0:T(8,128)S(1)}, f32[64,256]{1,0:T(8,128)S(1)}, u32[]{:S(2)}, u32[]{:S(2)}) collective-permute-start(f32[64,256]{1,0:T(8,128)S(1)} %get-tuple-element.60.refs_2_), channel_id=1, source_target_pairs={{1,0},{2,1},{3,2},{4,3},{5,4},{6,5},{7,6},{8,7},{9,8},{10,9},{11,1... | collective-permute-start | bytes 196616 | tf_op jit(solution)/shard_map/ppermute | solution.py:201
  97.9 7.7 %collective-permute-start.14 = (f32[64,256]{1,0:T(8,128)S(1)}, f32[64,256]{1,0:T(8,128)S(1)}, u32[]{:S(2)}, u32[]{:S(2)}) collective-permute-start(f32[64,256]{1,0:T(8,128)S(1)} %get-tuple-element.61.refs_3_), channel_id=1, source_target_pairs={{0,1},{1,2},{2,3},{3,4},{4,5},{5,6},{6,7},{7,8},{8,9},{9,10},{10,1... | collective-permute-start | bytes 196616 | tf_op jit(solution)/shard_map/ppermute | solution.py:200
